TPU v7x, 256 devices: a whole 4x4x8 slice. The times are simulated.
256 devices in a mesh: ctx: 16 (over y, x), tp: 8 (over z), dp: 2 (over core).
Axes of the slice: x: 4, y: 4, z: 8, core: 2. Of those that a mesh axis runs over, the one named last changes fastest.
Arguments:
- query_latent: bfloat16 [2, 2048, 32768], P('dp', 'ctx', 'tp'), may hold values from -120 to 120
- query_rotary: bfloat16 [2, 2048, 4096], P('dp', 'ctx', 'tp'), may hold values from -6 to 6
- key_latent: bfloat16 [2, 2048, 512], P('dp', 'ctx'), may hold values from -6 to 6
- key_rotary: bfloat16 [2, 2048, 64], P('dp', 'ctx'), may hold values from -6 to 6
- value_up: bfloat16 [64, 512, 128], P('tp', 'ctx'), may hold values from -0.25 to 0.25
- out_proj: bfloat16 [64, 128, 3584], P('tp', None, 'ctx'), may hold values from -0.0625 to 0.0625
- residual: bfloat16 [2, 2048, 3584], P('dp', ('ctx', 'tp')), may hold values from -0.59765625 to 0.59765625
- norm_gain: float32 [3584], replicated, may hold values from 0.1 to 1.9
- gate_proj: bfloat16 [128, 3584, 1024], P(('ctx', 'tp'), 'dp'), may hold values from -0.09375 to 0.09375
- up_proj: bfloat16 [128, 3584, 1024], P(('ctx', 'tp'), 'dp'), may hold values from -0.09375 to 0.09375
- down_proj: bfloat16 [128, 1024, 3584], P(('ctx', 'tp'), 'dp'), may hold values from -0.1875 to 0.1875
- expert_ids: int32 [2, 2048, 8], P('dp', ('ctx', 'tp')), may hold values from 0 to 127, all different within a row; in each aligned block of 16 rows (0 to 15, 16 to 31, ..., all dimensions but the last counted through in order) at most 2 rows name the same one
- route_score: float32 [2, 2048, 8], P('dp', ('ctx', 'tp')), may hold values from 0.05 to 1
- out_grad: bfloat16 [2, 2048, 3584], P('dp', ('ctx', 'tp')), may hold values from -6 to 6
Outputs:
- layer_out: bfloat16 [2, 2048, 3584], P('dp', ('ctx', 'tp'))
- resid_grad: bfloat16 [2, 2048, 3584], P('dp', ('ctx', 'tp'))
- score_grad: float32 [2, 2048, 8], P('dp', ('ctx', 'tp'))
Inputs may be any that keep to these rules, and one draw needn't show every extreme that they name: `expert_ids`: each token names 8 different experts. In each aligned block of 16 tokens of one sequence no expert is named by more than 2 tokens, a bound that some block reaches.
All inputs are finite; a program needn't handle non-finite values.
Results may differ from a plain program's by a relative error of at most 0.034.
Values may be sent and summed in bfloat16 or wider, within the bound.
A program may use at most 128 MiB of HBM per device.

v0:
```python
import jax
import jax.numpy as jnp
from jax import lax
from jax.sharding import PartitionSpec as P

route_scale = 2.5
norm_eps = 1e-06


def rms_scale(rows_in, norm_gain):
    inverse = lax.rsqrt(jnp.mean(rows_in * rows_in, axis=-1, keepdims=True) + norm_eps)
    return rows_in * inverse * norm_gain


def expert_pass(rows_u, rows_g, gate_w, up_w, down_w):
    act_a = jnp.dot(rows_u, gate_w, preferred_element_type=jnp.float32)
    act_b = jnp.dot(rows_u, up_w, preferred_element_type=jnp.float32)
    gated_act = jax.nn.silu(act_a)
    hidden = (gated_act * act_b).astype(jnp.bfloat16)
    result = jnp.dot(hidden, down_w, preferred_element_type=jnp.float32).astype(jnp.bfloat16)
    d_hidden = jnp.dot(rows_g, down_w.T, preferred_element_type=jnp.float32)
    sigmoid_a = jax.nn.sigmoid(act_a)
    slope_a = sigmoid_a * (1.0 + act_a * (1.0 - sigmoid_a))
    d_gate = (d_hidden * act_b * slope_a).astype(jnp.bfloat16)
    d_up = (d_hidden * gated_act).astype(jnp.bfloat16)
    d_rows = jnp.dot(d_gate, gate_w.T, preferred_element_type=jnp.float32) + jnp.dot(
        d_up, up_w.T, preferred_element_type=jnp.float32
    )
    return (result, d_rows.astype(jnp.bfloat16))


def head_outputs(latent_out, value_maps):
    rows_here, head_count = (latent_out.shape[1], latent_out.shape[0])
    mapped = jnp.einsum("hqc,hcv->qhv", latent_out, value_maps, preferred_element_type=jnp.float32)
    return mapped.astype(jnp.bfloat16).reshape(rows_here, head_count * value_maps.shape[2])


def per_device(
    query_latent,
    query_rotary,
    key_latent,
    key_rotary,
    value_up,
    out_proj,
    residual,
    norm_gain,
    gate_proj,
    up_proj,
    down_proj,
    expert_ids,
    route_score,
    out_grad,
):
    ctx_count = lax.axis_size("ctx")
    tp_count = lax.axis_size("tp")
    ctx_index = lax.axis_index("ctx")
    rows_here = query_latent.shape[1]
    head_count = value_up.shape[0]
    latent_width = key_latent.shape[2]
    rope_width = key_rotary.shape[2]
    value_width = value_up.shape[2]
    model_width = residual.shape[2]
    scale = (value_width + rope_width) ** (-0.5)
    queries = query_latent[0].reshape(rows_here, head_count, latent_width)
    rotary = query_rotary[0].reshape(rows_here, head_count, rope_width)
    query_pos = ctx_index * rows_here + jnp.arange(rows_here, dtype=jnp.int32)
    last_query = ctx_index * rows_here + rows_here - 1
    initial = (
        jnp.full((head_count, rows_here), -1e30, jnp.float32),
        jnp.zeros((head_count, rows_here), jnp.float32),
        jnp.zeros((head_count, rows_here, latent_width), jnp.float32),
    )
    pieces = (
        lax.all_gather(key_latent, "ctx", axis=1, tiled=True),
        lax.all_gather(key_rotary, "ctx", axis=1, tiled=True),
    )

    def compute(running):
        row_top, row_total, weighted = running
        key_block = pieces[0][0]
        rot_block = pieces[1][0]
        key_count = key_block.shape[0]
        scores = jnp.einsum("qhc,kc->hqk", queries, key_block, preferred_element_type=jnp.float32)
        scores = scores + jnp.einsum(
            "qhr,kr->hqk", rotary, rot_block, preferred_element_type=jnp.float32
        )
        key_pos = jnp.arange(key_count, dtype=jnp.int32)
        causal = key_pos[None, None, :] <= query_pos[None, :, None]
        scores = jnp.where(causal, scores * scale, -1e30)
        new_top = jnp.maximum(row_top, jnp.max(scores, axis=2))
        exp_terms = jnp.where(causal, jnp.exp(scores - new_top[:, :, None]), 0.0)
        row_total = jnp.sum(exp_terms, axis=2)
        weighted = jnp.einsum(
            "hqk,kc->hqc",
            exp_terms.astype(jnp.bfloat16),
            key_block,
            preferred_element_type=jnp.float32,
        )
        return (new_top, row_total, weighted)

    row_top, row_total, weighted = lax.cond(
        jnp.int32(0) <= last_query, compute, lambda running: running, initial
    )
    latent_out = (weighted / row_total[:, :, None]).astype(jnp.bfloat16)
    tok_rows = rows_here // tp_count
    value_maps, out_maps = (
        lax.all_gather(value_up, "ctx", axis=1, tiled=True),
        lax.all_gather(out_proj, "ctx", axis=2, tiled=True),
    )
    heads_out = head_outputs(latent_out, value_maps)
    flat_out = out_maps.reshape(head_count * value_width, model_width)
    attn_rows = lax.psum_scatter(
        jnp.dot(heads_out, flat_out, preferred_element_type=jnp.float32).astype(jnp.bfloat16),
        "tp",
        scatter_dimension=0,
        tiled=True,
    ).astype(jnp.float32)
    hidden_sum = residual[0].astype(jnp.float32) + attn_rows
    normed = rms_scale(hidden_sum, norm_gain).astype(jnp.bfloat16)
    route_ids = expert_ids[0]
    top_count = route_ids.shape[1]
    experts = ctx_count * tp_count
    capacity = 2 * tok_rows * top_count // experts
    flat_ids = route_ids.reshape(tok_rows * top_count)
    chosen = (flat_ids[:, None] == jnp.arange(experts, dtype=jnp.int32)[None, :]).astype(jnp.int32)
    earlier = jnp.cumsum(chosen, axis=0) - chosen
    slot_index = jnp.sum(earlier * chosen, axis=1)
    target = flat_ids * capacity + slot_index
    select = (target[:, None] == jnp.arange(experts * capacity, dtype=jnp.int32)[None, :]).astype(
        jnp.bfloat16
    )
    placing = jnp.sum(select.reshape(tok_rows, top_count, experts * capacity), axis=1)
    paired = jnp.concatenate([normed, out_grad[0]], axis=1)
    outgoing = jnp.dot(placing.T, paired, preferred_element_type=jnp.float32).astype(jnp.bfloat16)
    outgoing = outgoing.reshape(experts, capacity, 2, model_width)
    gate_full, up_full, down_full = (
        lax.all_gather(gate_proj, "dp", axis=1, tiled=True),
        lax.all_gather(up_proj, "dp", axis=1, tiled=True),
        lax.all_gather(down_proj, "dp", axis=1, tiled=True),
    )
    gate_w = gate_full[0]
    up_w = up_full[0]
    down_w = down_full[0]
    arrived = lax.all_to_all(outgoing, ("ctx", "tp"), split_axis=0, concat_axis=0, tiled=True)
    sources = arrived.shape[0]
    slot_count = arrived.shape[1]
    slot_rows = arrived.reshape(sources * slot_count, 2, model_width)
    result, d_rows = expert_pass(slot_rows[:, 0], slot_rows[:, 1], gate_w, up_w, down_w)
    going_back = jnp.stack([result, d_rows], axis=1).reshape(sources, slot_count, 2, model_width)
    returned = lax.all_to_all(going_back, ("ctx", "tp"), split_axis=0, concat_axis=0, tiled=True)
    per_route = jnp.dot(
        select,
        returned.reshape(experts * capacity, 2 * model_width),
        preferred_element_type=jnp.float32,
    )
    per_route = per_route.reshape(tok_rows, top_count, 2, model_width)
    route_out = per_route[:, :, 0]
    route_grad = per_route[:, :, 1]
    route_raw = route_score[0]
    score_total = jnp.sum(route_raw, axis=1, keepdims=True)
    route_weight = route_scale * route_raw / score_total
    mixed_out = hidden_sum + jnp.einsum(
        "tk,tkd->td", route_weight, route_out, precision=lax.Precision.HIGHEST
    )
    grad_rows = out_grad[0].astype(jnp.float32)
    weight_grad = jnp.einsum("td,tkd->tk", grad_rows, route_out, precision=lax.Precision.HIGHEST)
    d_normed = jnp.einsum("tk,tkd->td", route_weight, route_grad, precision=lax.Precision.HIGHEST)
    unused, pullback = jax.vjp(lambda rows_in: rms_scale(rows_in, norm_gain), hidden_sum)
    resid_grad = (grad_rows + pullback(d_normed)[0]).astype(jnp.bfloat16)
    score_grad = (
        route_scale
        / score_total
        * (weight_grad - jnp.sum(weight_grad * route_raw, axis=1, keepdims=True) / score_total)
    )
    return (mixed_out.astype(jnp.bfloat16)[None], resid_grad[None], score_grad[None])


def solution(mesh):
    return jax.shard_map(
        per_device,
        mesh=mesh,
        in_specs=(
            P("dp", "ctx", "tp"),
            P("dp", "ctx", "tp"),
            P("dp", "ctx", None),
            P("dp", "ctx", None),
            P("tp", "ctx", None),
            P("tp", None, "ctx"),
            P("dp", ("ctx", "tp"), None),
            P(),
            P(("ctx", "tp"), "dp", None),
            P(("ctx", "tp"), "dp", None),
            P(("ctx", "tp"), "dp", None),
            P("dp", ("ctx", "tp"), None),
            P("dp", ("ctx", "tp"), None),
            P("dp", ("ctx", "tp"), None),
        ),
        out_specs=(
            P("dp", ("ctx", "tp"), None),
            P("dp", ("ctx", "tp"), None),
            P("dp", ("ctx", "tp"), None),
        ),
        check_vma=False,
    )
```

profile of v0, /device:TPU:32, one launch (start us, length us, event | category | flops | bytes accessed | tf_op | source)
XLA Modules:
  0.0 521.7 jit_solution(13411717028966328108)
XLA Ops:
  8.0 0.7 all-gather.7.cloned.1.call-update
  8.7 0.0 all-gather.9.cloned.1.call-start
  8.8 0.7 all-gather.9.cloned.1.call-update
  9.5 0.7 all-gather.11.cloned.1.call-update
  10.2 0.0 reduce-scatter.2.cloned.1.call-start
  10.3 24.5 %all_gather.22 = bf16[1,2048,64]{1,2,0:T(8,128)(2,1)S(1)} all-gather(bf16[1,128,64]{1,2,0:T(8,128)(2,1)} %param.19), channel_id=1, replica_groups=mesh['ctx'=16,'tp'=8,'dp'=2] {'ctx'}, dimensions={1}, use_global_device_ids=true | all-gather | bytes 278528 | tf_op jit(solution)/shard_map/all_gather | solution.py:75
  34.7 29.1 %all-gather.7.cloned.1.call-done = bf16[1,2048,512]{2,1,0:T(8,128)(2,1)} async-done(((bf16[1,128,512]{2,1,0:T(8,128)(2,1)}), bf16[1,2048,512]{2,1,0:T(8,128)(2,1)}) %all-gather.7.cloned.1.call-update) | async-done | bytes 2097168 | tf_op jit(solution)/shard_map/all_gather | solution.py:74
  63.8 17.5 %conditional.1 = (f32[8,128]{1,0:T(8,128)S(1)}, f32[8,128,512]{2,1,0:T(8,128)S(1)}) conditional(s32[]{:T(128)} %convert_element_type.68, () %tuple.16, (s32[]{:T(128)}, s32[128]{0:T(128)S(1)}, bf16[1,2048,512]{2,1,0:T(8,128)(2,1)}, bf16[1,128,4096]{2,1,0:T(8,128)(2,1)}, bf16[1,2048,64]{1,2,0:T(8,128)(2,1)S(1)}, ...), branch_computations={%region_0.0_spmd, %region_1.4_spmd} | conditional | flops 4584635392 | bytes 62023244 | solution.py:101
  63.9 0.2 iota_compare_fusion
  64.0 1.6 copy.58
  65.7 6.4 %fusion.8 = f32[2048,128,8]{1,0,2:T(8,128)} fusion(bf16[1,2048,512]{2,1,0:T(8,128)(2,1)} %get-tuple-element.18, bf16[128,8,512]{2,1,0:T(8,128)(2,1)S(1)} %bitcast.136), kind=kOutput, calls=%fused_computation.9 | convolution fusion | flops 2147483648 | bytes 11534336 | tf_op jit(solution)/shard_map/cond/branch_1_fun/qhc,kc->hqk/dot_general | solution.py:83
  72.1 0.1 copy.39
  72.2 5.2 fusion.69
  77.4 2.4 fusion.2
  79.9 1.4 fusion.1
  81.3 32.7 %all-gather.9.cloned.1.call-done = bf16[8,512,128]{2,1,0:T(8,128)(2,1)} async-done(((bf16[8,32,128]{2,1,0:T(8,128)(2,1)}), bf16[8,512,128]{2,1,0:T(8,128)(2,1)}) %all-gather.9.cloned.1.call-update) | async-done | bytes 1048592 | tf_op jit(solution)/shard_map/all_gather | solution.py:107
  114.0 73.1 %all-gather.11.cloned.1.call-done = bf16[8,128,3584]{1,2,0:T(8,128)(2,1)} async-done(((bf16[8,128,224]{1,2,0:T(8,128)(2,1)}), bf16[8,128,3584]{1,2,0:T(8,128)(2,1)}) %all-gather.11.cloned.1.call-update) | async-done | bytes 7340048 | tf_op jit(solution)/shard_map/all_gather | solution.py:108
  187.1 7.2 %fusion.34 = bf16[128,3584]{1,0:T(8,128)(2,1)} fusion(bf16[8,128,3584]{1,2,0:T(8,128)(2,1)} %all-gather.11.cloned.1.call-done, bf16[8,512,128]{2,1,0:T(8,128)(2,1)} %all-gather.9.cloned.1.call-done, f32[8,128,512]{2,1,0:T(8,128)S(1)} %get-tuple-element.27, f32[8,128]{1,0:T(8,128)S(1)} %get-tuple-element.28), kind=kOutput, calls=%fused_computation.34 | convolution fusion | flops 1075380224 | bytes 11407360 | tf_op jit(solution)/shard_map/dot_general | solution.py:113
  194.4 0.0 all-gather.13.cloned.1.call-start
  194.5 0.5 all-gather.13.cloned.1.call-update
  195.0 11.6 %all-gather.15.cloned.1.call-start = ((), (), s32[]{:S(2)}) async-start(), calls=%async_computation.8 | async-start | bytes 11010048 | tf_op jit(solution)/shard_map/all_gather | solution.py:138
  206.6 0.1 copy.40
  206.7 0.1 eq.51
  206.8 0.1 fusion.58
  206.9 0.2 reduce_window_sum.11
  207.1 0.2 select_reduce_fusion
  207.3 0.1 reduce_sum.78
  207.3 0.1 copy.41
  207.4 0.1 copy.42
  207.5 0.1 fusion.56
  207.6 24.1 %reduce-scatter.2.cloned.1.call-done = bf16[16,3584]{1,0:T(8,128)(2,1)} async-done(((bf16[128,3584]{1,0:T(8,128)(2,1)}), bf16[16,3584]{1,0:T(8,128)(2,1)}) %reduce-scatter.2.cloned.1.call-update) | async-done | bytes 114704 | tf_op jit(solution)/shard_map/reduce_scatter | solution.py:112
  231.7 1.0 multiply_reduce_fusion.1
  232.8 1.0 multiply_convert_fusion.6
  233.8 3.0 convolution_convert_fusion
  236.8 9.5 %reshape.124 = bf16[128,2,2,3584]{3,2,1,0:T(2,128)(2,1)} reshape(bf16[256,7168]{1,0:T(8,128)(2,1)} %convolution_convert_fusion) | data formatting | bytes 7340032 | tf_op jit(solution)/shard_map/reshape | solution.py:135
  246.3 12.2 %all-to-all-start = ((bf16[128,2,2,3584]{3,2,1,0:T(2,128)(2,1)}), bf16[128,2,2,3584]{3,2,1,0:T(2,128)(2,1)}, u32[]{:S(2)}, u32[]{:S(2)}) async-start(bf16[128,2,2,3584]{3,2,1,0:T(2,128)(2,1)} %reshape.124), calls=%async_computation.1 | async-start | bytes 7340032 | tf_op jit(solution)/shard_map/all_to_all | solution.py:144
  258.4 0.0 all-gather.17.cloned.1.call-start
  258.5 0.5 all-gather.17.cloned.1.call-update
  259.0 82.3 %all-to-all-done = bf16[128,2,2,3584]{3,2,1,0:T(2,128)(2,1)} async-done(((bf16[128,2,2,3584]{3,2,1,0:T(2,128)(2,1)}), bf16[128,2,2,3584]{3,2,1,0:T(2,128)(2,1)}, u32[]{:S(2)}, u32[]{:S(2)}) %all-to-all-start) | async-done | bytes 3670048 | tf_op jit(solution)/shard_map/all_to_all | solution.py:144
  341.3 8.9 %fusion.70 = (bf16[256,1,3584]{2,1,0:T(2,128)(2,1)}, bf16[256,1,3584]{2,1,0:T(2,128)(2,1)}) fusion(bf16[256,2,3584]{2,1,0:T(2,128)(2,1)} %bitcast.16), kind=kLoop, calls=%fused_computation.96 | loop fusion | bytes 7340032 | tf_op jit(solution)/shard_map/slice | solution.py:148
  350.2 6.3 %fusion.23 = f32[256,1024]{1,0:T(8,128)S(1)} fusion(bf16[1,3584,1024]{2,1,0:T(8,128)(2,1)} %all-gather.13.cloned.1.call-done, bf16[256,1,3584]{2,1,0:T(2,128)(2,1)} %get-tuple-element.53), kind=kOutput, calls=%fused_computation.28 | convolution fusion | flops 1879048192 | bytes 10223616 | tf_op jit(solution)/shard_map/dot_general | solution.py:16
  356.5 7.3 %fusion.19 = f32[256,1024]{1,0:T(8,128)} fusion(bf16[1,3584,1024]{2,1,0:T(8,128)(2,1)} %all-gather.15.cloned.1.call-done, bf16[256,1,3584]{2,1,0:T(2,128)(2,1)} %get-tuple-element.53), kind=kOutput, calls=%fused_computation.24 | convolution fusion | flops 1879048192 | bytes 10223616 | tf_op jit(solution)/shard_map/dot_general | solution.py:17
  363.8 6.4 %fusion.13 = f32[256,1024]{1,0:T(8,128)S(1)} fusion(bf16[1,1024,3584]{2,1,0:T(8,128)(2,1)} %all-gather.17.cloned.1.call-done, bf16[256,1,3584]{2,1,0:T(2,128)(2,1)} %get-tuple-element.54), kind=kOutput, calls=%fused_computation.18 | convolution fusion | flops 1879048192 | bytes 10223616 | tf_op jit(solution)/shard_map/dot_general | solution.py:21
  370.2 1.0 copy-done.10
  371.2 2.2 fusion.17
  373.4 3.9 fusion.31
  377.3 3.7 stack.13
  381.0 5.5 %fusion.28 = bf16[256,3584]{1,0:T(8,128)(2,1)S(1)} fusion(bf16[1,1024,3584]{2,1,0:T(8,128)(2,1)} %all-gather.17.cloned.1.call-done, f32[256,1024]{1,0:T(8,128)} %fusion.19, f32[256,1024]{1,0:T(8,128)S(1)} %fusion.23), kind=kOutput, calls=%fused_computation.31 | convolution fusion | flops 1881538560 | bytes 11272192 | tf_op jit(solution)/shard_map/dot_general | solution.py:20
  386.5 3.8 stack.12
  390.3 9.8 %pad_maximum_fusion = bf16[128,2,2,3584]{3,2,1,0:T(2,128)(2,1)} fusion(bf16[128,2,1,3584]{3,2,1,0:T(2,128)(2,1)} %stack.13, bf16[128,2,1,3584]{3,2,1,0:T(2,128)(2,1)} %stack.12), kind=kLoop, calls=%fused_computation.35 | loop fusion | flops 7340032 | bytes 7340032 | tf_op jit(solution)/shard_map/stack | solution.py:149
  400.1 7.8 %all-to-all-start.1 = ((bf16[128,2,2,3584]{3,2,1,0:T(2,128)(2,1)}), bf16[128,2,2,3584]{3,2,1,0:T(2,128)(2,1)}, u32[]{:S(2)}, u32[]{:S(2)}) async-start(bf16[128,2,2,3584]{3,2,1,0:T(2,128)(2,1)} %pad_maximum_fusion), calls=%async_computation.2 | async-start | bytes 7340032 | tf_op jit(solution)/shard_map/all_to_all | solution.py:150
  408.0 80.6 %all-to-all-done.1 = bf16[128,2,2,3584]{3,2,1,0:T(2,128)(2,1)} async-done(((bf16[128,2,2,3584]{3,2,1,0:T(2,128)(2,1)}), bf16[128,2,2,3584]{3,2,1,0:T(2,128)(2,1)}, u32[]{:S(2)}, u32[]{:S(2)}) %all-to-all-start.1) | async-done | bytes 3670048 | tf_op jit(solution)/shard_map/all_to_all | solution.py:150
  488.6 4.4 copy.59
  493.0 5.9 %copy.47 = bf16[7168,256]{1,0:T(8,128)(2,1)} copy(bf16[7168,256]{0,1:T(8,128)(2,1)} %bitcast.133) | data formatting | bytes 7340032 | tf_op jit(solution)/shard_map/dot_general | solution.py:151
  499.0 3.4 fusion.51
  502.4 1.8 copy-done
  504.1 1.9 fusion.36
  506.1 0.1 copy.54
  506.2 0.1 copy.50
  506.2 3.1 fusion.37
  509.3 3.1 fusion.35
  512.5 0.2 multiply_reduce_fusion
  512.6 0.6 fusion.61
  513.2 0.8 fusion.55
  (41 shorter events, 0.3 us)
Async XLA Ops:
  8.0 55.8 %all-gather.7.cloned.1.call-start = ((), (), s32[]{:S(2)}) async-start(), calls=%async_computation.3 | async-start | bytes 2228224 | tf_op jit(solution)/shard_map/all_gather | solution.py:74
  8.7 105.3 %all-gather.9.cloned.1.call-start = ((), (), s32[]{:S(2)}) async-start(), calls=%async_computation.4 | async-start | bytes 1114112 | tf_op jit(solution)/shard_map/all_gather | solution.py:107
  9.5 177.6 %all-gather.11.cloned.1.call-start = ((), (), s32[]{:S(2)}) async-start(), calls=%async_computation.5 | async-start | bytes 7798784 | tf_op jit(solution)/shard_map/all_gather | solution.py:108
  10.2 221.5 %reduce-scatter.2.cloned.1.call-start = ((), (), s32[]{:S(2)}) async-start(), calls=%async_computation.6 | async-start | bytes 1032192 | tf_op jit(solution)/shard_map/reduce_scatter | solution.py:112
  65.7 6.4 %copy-start.5 = (bf16[1,128,512]{2,1,0:T(8,128)(2,1)S(1)}, bf16[1,128,512]{2,1,0:T(8,128)(2,1)}, u32[]{:S(2)}) copy-start(bf16[1,128,512]{2,1,0:T(8,128)(2,1)} %get-tuple-element.50) | copy-start | bytes 393220 | tf_op jit(solution)/shard_map/cond
  72.2 5.2 %copy-start.9 = (bf16[1,2048,512]{2,1,0:T(8,128)(2,1)S(1)}, bf16[1,2048,512]{2,1,0:T(8,128)(2,1)}, u32[]{:S(2)}) copy-start(bf16[1,2048,512]{2,1,0:T(8,128)(2,1)} %get-tuple-element.18) | copy-start | bytes 6291460 | tf_op jit(solution)/shard_map/cond
  194.4 12.3 %copy-start.6 = (s32[1,16,8]{1,2,0:T(8,128)S(1)}, s32[1,16,8]{1,2,0:T(8,128)}, u32[]{:S(2)}) copy-start(s32[1,16,8]{1,2,0:T(8,128)} %param.27) | copy-start | bytes 1540
  194.4 37.4 %copy-start.1 = (bf16[1,16,3584]{2,1,0:T(8,128)(2,1)S(1)}, bf16[1,16,3584]{2,1,0:T(8,128)(2,1)}, u32[]{:S(2)}) copy-start(bf16[1,16,3584]{2,1,0:T(8,128)(2,1)} %param.22) | copy-start | bytes 344068
  194.4 38.4 %copy-start.4 = (f32[3584]{0:T(1024)S(1)}, f32[3584]{0:T(1024)}, u32[]{:S(2)}) copy-start(f32[3584]{0:T(1024)} %param.23) | copy-start | bytes 43012
  194.4 39.4 %copy-start.3 = (bf16[1,16,3584]{2,1,0:T(8,128)(2,1)S(1)}, bf16[1,16,3584]{2,1,0:T(8,128)(2,1)}, u32[]{:S(2)}) copy-start(bf16[1,16,3584]{2,1,0:T(8,128)(2,1)} %param.29) | copy-start | bytes 344068
  194.4 155.8 %all-gather.13.cloned.1.call-start = ((), (), s32[]{:S(2)}) async-start(), calls=%async_computation.7 | async-start | bytes 11010048 | tf_op jit(solution)/shard_map/all_gather | solution.py:137
  195.0 161.5 %all-gather.15.cloned.1.call-start = ((), (), s32[]{:S(2)}) async-start(), calls=%async_computation.8 | async-start | bytes 11010048 | tf_op jit(solution)/shard_map/all_gather | solution.py:138
  246.3 95.0 %all-to-all-start = ((bf16[128,2,2,3584]{3,2,1,0:T(2,128)(2,1)}), bf16[128,2,2,3584]{3,2,1,0:T(2,128)(2,1)}, u32[]{:S(2)}, u32[]{:S(2)}) async-start(bf16[128,2,2,3584]{3,2,1,0:T(2,128)(2,1)} %reshape.124), calls=%async_computation.1 | async-start | bytes 7340032 | tf_op jit(solution)/shard_map/all_to_all | solution.py:144
  258.4 105.3 %all-gather.17.cloned.1.call-start = ((), (), s32[]{:S(2)}) async-start(), calls=%async_computation.9 | async-start | bytes 11010048 | tf_op jit(solution)/shard_map/all_gather | solution.py:139
  363.8 7.4 %copy-start.8 = (bf16[1,3584,1024]{2,1,0:T(8,128)(2,1)S(1)}, bf16[1,3584,1024]{2,1,0:T(8,128)(2,1)}, u32[]{:S(2)}) copy-start(bf16[1,3584,1024]{2,1,0:T(8,128)(2,1)} %all-gather.15.cloned.1.call-done) | copy-start | bytes 22020100
  363.8 9.6 %slice-start = ((s8[7340032]{0:T(1024)(128)(4,1)}), s8[4194304]{0:T(1024)(128)(4,1)S(1)}, s32[]{:S(2)}) async-start(s8[7340032]{0:T(1024)(128)(4,1)} %bitcast.140), calls=%async_computation.10 | async-start | bytes 8388608
  370.2 1.0 copy-start.10
  371.2 2.2 slice-start.1
  400.1 7.8 %copy-start.7 = (f32[1,16,8]{1,2,0:T(8,128)S(1)}, f32[1,16,8]{1,2,0:T(8,128)}, u32[]{:S(2)}) copy-start(f32[1,16,8]{1,2,0:T(8,128)} %param.28) | copy-start | bytes 1540
  400.1 88.5 %all-to-all-start.1 = ((bf16[128,2,2,3584]{3,2,1,0:T(2,128)(2,1)}), bf16[128,2,2,3584]{3,2,1,0:T(2,128)(2,1)}, u32[]{:S(2)}, u32[]{:S(2)}) async-start(bf16[128,2,2,3584]{3,2,1,0:T(2,128)(2,1)} %pad_maximum_fusion), calls=%async_computation.2 | async-start | bytes 7340032 | tf_op jit(solution)/shard_map/all_to_all | solution.py:150
  502.3 1.8 copy-start
  502.3 10.1 %copy-start.2 = (bf16[16,3584]{1,0:T(8,128)(2,1)S(1)}, bf16[16,3584]{1,0:T(8,128)(2,1)}, u32[]{:S(2)}) copy-start(bf16[16,3584]{1,0:T(8,128)(2,1)} %reduce-scatter.2.cloned.1.call-done) | copy-start | bytes 344068
Sparse Core Ops, SparseCore 0:
  11.3 52.5 all-gather.6
  66.2 47.7 all-gather.8
  116.5 70.5 all-gather.10
  194.5 37.1 reduce-scatter.1
Sparse Core Ops, SparseCore 1:
  196.8 23.3 all-gather.12
  221.9 24.8 all-gather.14
  260.8 24.9 all-gather.16
where the time goes:
time: 530 us; the launch traced here: 522 us
  waiting for transfers between devices  325 us (61%)
  matrix products  67.2 us (13%)
  local copies, waits for them, and re-layouts  41.3 us (8%)
  starting transfers between devices  31.9 us (6%)
  blocking collectives  24.5 us (5%)
  between operations  16.1 us (3%)
  other arithmetic  15.6 us (3%)
    all_to_all x1, waiting for transfers between devices, per_device(): lax.all_to_all(outgoing, ('ctx', 'tp'), split_axis=0, concat_axis=0, tile...  82.3 us
    all_to_all x1, waiting for transfers between devices, per_device(): lax.all_to_all(going_back, ('ctx', 'tp'), split_axis=0, concat_axis=0, ti...  80.6 us
    all_gather x1, waiting for transfers between devices, per_device(): lax.all_gather(out_proj, 'ctx', axis=2, tiled=True)  73.1 us
    all_gather x1, waiting for transfers between devices, per_device(): lax.all_gather(value_up, 'ctx', axis=1, tiled=True)  32.7 us
    all_gather x1, waiting for transfers between devices, per_device(): lax.all_gather(key_latent, 'ctx', axis=1, tiled=True)  29.1 us
    all_gather x1, blocking collectives, per_device(): lax.all_gather(key_rotary, 'ctx', axis=1, tiled=True)  24.5 us
    reduce_scatter x1, waiting for transfers between devices, per_device(): lax.psum_scatter(jnp.dot(heads_out, flat_out, preferred_element_type=jnp....  24.1 us
    all_to_all x1, starting transfers between devices, per_device(): lax.all_to_all(outgoing, ('ctx', 'tp'), split_axis=0, concat_axis=0, tile...  12.2 us
  transfers between devices with their start and end apart: 9, of which 6 were waited for; matrix products, arithmetic and copies ran while one was open for 11% of the time, Pallas kernels for 0%

commit v1 on v0

v1 whole, which is shorter than its diff:
```python
import functools

import jax
import jax.numpy as jnp
from jax import lax
from jax.experimental import pallas as pl
from jax.experimental.pallas import tpu as pltpu
from jax.sharding import PartitionSpec as P

MESH = pl.DeviceIdType.MESH
f32 = jnp.float32
bf16 = jnp.bfloat16
route_scale = 2.5
norm_eps = 1e-06
CAP = 2


def remote(src, dst, send_sem, recv_sem, device):
    return pltpu.make_async_remote_copy(
        src_ref=src, dst_ref=dst, send_sem=send_sem, recv_sem=recv_sem, device_id=device, device_id_type=MESH
    )


def each_peer(n, fn):
    def body(off, carry):
        fn(off)
        return carry

    lax.fori_loop(1, n, body, 0)


def each(lo, hi, fn):
    def body(i, carry):
        fn(i)
        return carry

    lax.fori_loop(lo, hi, body, 0)


def nt(a, b):
    return lax.dot_general(a, b, (((1,), (1,)), ((), ())), preferred_element_type=f32)


def nn(a, b):
    return lax.dot_general(a, b, (((1,), (0,)), ((), ())), preferred_element_type=f32)


def tn(a, b):
    return lax.dot_general(a, b, (((0,), (0,)), ((), ())), preferred_element_type=f32)


def attn_kernel(
    C, T,
    ql, qr, kl, kr, vs, os_, res, gain, gw, uw, dw,
    hs_o, nm_o, go, uo, do,
    qbuf, kbuf, sbuf, vbuf, obuf, lat, heads, part, rsb,
    w_ss, w_rs, k_ss, k_rs, v_ss, v_rs, o_ss, o_rs, sv_ss, sv_rs, so_ss, so_rs, r_ss, r_rs,
):
    c, t, d = lax.axis_index("ctx"), lax.axis_index("tp"), lax.axis_index("dp")
    rows = ql.shape[0]
    H, LR, VD = vs.shape
    LAT = kl.shape[1]
    ROPE = kr.shape[1]
    KW = kbuf.shape[1]
    OC = os_.shape[2]
    OH = OC // 2
    Hh = H // 2
    tok, D = res.shape
    scale = (VD + ROPE) ** (-0.5)
    sib = {"dp": 1 - d}

    bar = pltpu.get_barrier_semaphore()
    each_peer(C, lambda o: pl.semaphore_signal(bar, inc=1, device_id={"ctx": lax.rem(c + o, C)}, device_id_type=MESH))
    each_peer(T, lambda o: pl.semaphore_signal(bar, inc=1, device_id={"tp": lax.rem(t + o, T)}, device_id_type=MESH))
    pl.semaphore_signal(bar, inc=1, device_id=sib, device_id_type=MESH)

    my_keys = pl.ds(pl.multiple_of(c * rows, rows), rows)
    kbuf[my_keys, 0:LAT] = kl[...]
    kbuf[my_keys, LAT:KW] = jnp.concatenate([kr[...], jnp.zeros((rows, KW - LAT - ROPE), bf16)], axis=1)
    pl.semaphore_wait(bar, C + T - 1)

    def key_rows(i):
        return kbuf.at[pl.ds(pl.multiple_of(i * rows, rows), rows)]

    each(c + 1, C, lambda j: remote(key_rows(c), key_rows(c), k_ss.at[j], k_rs.at[c], {"ctx": j}).start())

    swaps = [remote(a, b, w_ss.at[i], w_rs.at[i], sib) for i, (a, b) in enumerate(((gw, go), (uw, uo), (dw, do)))]
    for s in swaps:
        s.start()

    eye = (
        lax.broadcasted_iota(jnp.int32, (OC, OC), 0) == lax.broadcasted_iota(jnp.int32, (OC, OC), 1)
    ).astype(bf16)
    obuf[pl.ds(pl.multiple_of(c * OC, OC), OC), :] = nt(eye, os_[...].reshape(H * VD, OC)).astype(bf16)
    vbuf[:, pl.ds(pl.multiple_of(c * LR, LR), LR), :] = vs[...]

    def v_part(owner, half):
        return vbuf.at[pl.ds(half * Hh, Hh), pl.ds(pl.multiple_of(owner * LR, LR), LR), :]

    def o_part(owner, half):
        return obuf.at[pl.ds(pl.multiple_of(owner * OC + half * OH, OH), OH), :]

    def send_vo(off):
        p = lax.rem(c + off, C)
        remote(o_part(c, d), o_part(c, d), o_ss.at[p], o_rs.at[c], {"ctx": p}).start()
        remote(v_part(c, d), v_part(c, d), v_ss.at[p], v_rs.at[c], {"ctx": p}).start()

    each_peer(C, send_vo)

    def blank(j):
        kbuf[pl.ds(pl.multiple_of(j * rows, rows), rows), :] = jnp.zeros((rows, KW), bf16)

    each(c + 1, C, blank)
    for h in range(H):
        qbuf[h * rows : (h + 1) * rows, 0:LAT] = ql[:, h * LAT : (h + 1) * LAT]
        qbuf[h * rows : (h + 1) * rows, LAT:KW] = jnp.concatenate(
            [qr[:, h * ROPE : (h + 1) * ROPE], jnp.zeros((rows, KW - LAT - ROPE), bf16)], axis=1
        )

    each(0, c, lambda j: remote(key_rows(j), key_rows(j), k_ss.at[j], k_rs.at[j], {"ctx": j}).wait_recv())

    S = C * rows
    NB = 4 if S % 4 == 0 else 1
    SN = S // NB
    MB = 2 * rows

    def attend(i):
        r = pl.ds(pl.multiple_of(i * MB, MB), MB)
        q = qbuf[r, :]
        qpos = c * rows + lax.rem(lax.broadcasted_iota(jnp.int32, (MB, SN), 0), rows)
        kpos = lax.broadcasted_iota(jnp.int32, (MB, SN), 1)
        top = jnp.full((MB, 1), -1e30, f32)
        for n in range(NB):
            s = nt(q, kbuf[n * SN : (n + 1) * SN, :]) * scale
            s = jnp.where(kpos + n * SN <= qpos, s, -1e30)
            sbuf[:, n * SN : (n + 1) * SN] = s
            top = jnp.maximum(top, jnp.max(s, axis=1, keepdims=True))
        total = jnp.zeros((MB, 1), f32)
        acc = jnp.zeros((MB, LAT), f32)
        for n in range(NB):
            p = jnp.exp(sbuf[:, n * SN : (n + 1) * SN] - top)
            total = total + jnp.sum(p, axis=1, keepdims=True)
            acc = acc + nn(p.astype(bf16), kbuf[n * SN : (n + 1) * SN, 0:LAT])
        lat[r, :] = (acc / total).astype(bf16)

    each(0, H // 2, attend)

    def relay(off):
        p = lax.rem(c + C - off, C)
        remote(o_part(p, d), o_part(p, d), o_ss.at[p], o_rs.at[p], {"ctx": p}).wait_recv()
        remote(o_part(p, d), o_part(p, d), so_ss.at[p], so_rs.at[p], sib).start()
        remote(v_part(p, d), v_part(p, d), v_ss.at[p], v_rs.at[p], {"ctx": p}).wait_recv()
        remote(v_part(p, d), v_part(p, d), sv_ss.at[p], sv_rs.at[p], sib).start()

    each_peer(C, relay)

    def relayed(off):
        p = lax.rem(c + C - off, C)
        remote(o_part(p, 1 - d), o_part(p, 1 - d), so_ss.at[p], so_rs.at[p], sib).wait_recv()
        remote(v_part(p, 1 - d), v_part(p, 1 - d), sv_ss.at[p], sv_rs.at[p], sib).wait_recv()

    each_peer(C, relayed)

    for h in range(H):
        heads[:, h * VD : (h + 1) * VD] = nn(lat[h * rows : (h + 1) * rows, :], vbuf[h]).astype(bf16)

    PN = 512 if D % 512 == 0 else D

    def project(n):
        cols = pl.ds(pl.multiple_of(n * PN, PN), PN)
        part[:, :, cols] = nt(heads[...], obuf[cols, :]).astype(bf16).reshape(T, tok, PN)

    each(0, D // PN, project)

    def send_part(off):
        p = lax.rem(t + off, T)
        remote(part.at[p], rsb.at[t], r_ss.at[p], r_rs.at[t], {"tp": p}).start()

    each_peer(T, send_part)
    rsb[t] = part[t]

    def got_part(off):
        p = lax.rem(t + T - off, T)
        remote(part.at[p], rsb.at[p], r_ss.at[p], r_rs.at[p], {"tp": p}).wait_recv()

    each_peer(T, got_part)
    hs = rsb[0].astype(f32)
    for i in range(1, T):
        hs = hs + rsb[i].astype(f32)
    hs = hs + res[...].astype(f32)
    hs_o[...] = hs
    inv = lax.rsqrt(jnp.mean(hs * hs, axis=1, keepdims=True) + norm_eps)
    nm_o[...] = (hs * inv * gain[...]).astype(bf16)

    each(c + 1, C, lambda j: remote(key_rows(c), key_rows(c), k_ss.at[j], k_rs.at[c], {"ctx": j}).wait_send())

    def sent(off):
        p = lax.rem(c + off, C)
        remote(o_part(c, d), o_part(c, d), o_ss.at[p], o_rs.at[c], {"ctx": p}).wait_send()
        remote(v_part(c, d), v_part(c, d), v_ss.at[p], v_rs.at[c], {"ctx": p}).wait_send()
        remote(o_part(p, d), o_part(p, d), so_ss.at[p], so_rs.at[p], sib).wait_send()
        remote(v_part(p, d), v_part(p, d), sv_ss.at[p], sv_rs.at[p], sib).wait_send()

    each_peer(C, sent)

    def part_sent(off):
        p = lax.rem(t + off, T)
        remote(part.at[p], rsb.at[t], r_ss.at[p], r_rs.at[t], {"tp": p}).wait_send()

    each_peer(T, part_sent)
    for s in swaps:
        s.wait()


def moe_kernel(
    C, T, K, ND, NR,
    u, g, meta, hs, gain, gw, uw, dw, go, uo, do,
    lo_o, rg_o, sg_o,
    gs, us, ds_, zu, zg, zm, su, sg, au, ag, act, ro, rd, rw, bo, bd, bw, po, pd, pw, fo, fd, fw,
    wl, z_ss, z_rs, x_ss, x_rs, b_ss, b_rs, bw_ss, bw_rs, y_ss, y_rs, yw_ss, yw_rs,
):
    c, t, d = lax.axis_index("ctx"), lax.axis_index("tp"), lax.axis_index("dp")
    tok, D = u.shape
    DH = gw.shape[0]
    HH = dw.shape[0]
    HID = 2 * HH
    SL = CAP * T
    NT = T * tok
    NS = C * SL
    CD, CR = D // ND, D // NR

    loads = []
    for i, (own, other, dst, n) in enumerate(((dw, do, ds_, HH), (gw, go, gs, DH), (uw, uo, us, DH))):
        loads.append(pltpu.make_async_copy(own, dst.at[pl.ds(pl.multiple_of(d * n, n), n)], wl.at[i, 0]))
        loads.append(pltpu.make_async_copy(other, dst.at[pl.ds(pl.multiple_of((1 - d) * n, n), n)], wl.at[i, 1]))
    for s in loads:
        s.start()

    bar = pltpu.get_barrier_semaphore()
    each_peer(C, lambda o: pl.semaphore_signal(bar, inc=1, device_id={"ctx": lax.rem(c + o, C)}, device_id_type=MESH))
    each_peer(T, lambda o: pl.semaphore_signal(bar, inc=1, device_id={"tp": lax.rem(t + o, T)}, device_id_type=MESH))
    zu[t] = u[...]
    zg[t] = g[...]
    zm[t] = meta[...]
    pl.semaphore_wait(bar, C + T - 2)

    zs = (zm, zg, zu)
    for i, z in enumerate(zs):
        each_peer(
            T,
            lambda o: remote(
                z.at[t], z.at[t], z_ss.at[i, lax.rem(t + o, T)], z_rs.at[i, t], {"tp": lax.rem(t + o, T)}
            ).start(),
        )

    def z_wait(i):
        def one(off):
            p = lax.rem(t + T - off, T)
            remote(zs[i].at[p], zs[i].at[p], z_ss.at[i, p], z_rs.at[i, p], {"tp": p}).wait_recv()

        each_peer(T, one)

    z_wait(0)
    m = zm[...].reshape(NT, zm.shape[2])
    lane = lax.broadcasted_iota(jnp.int32, (NT, NS), 1)
    wanted = (lax.div(lane, SL) * T + t).astype(f32)
    slot = lax.rem(lane, SL).astype(f32)
    scores = [m[:, K + k : K + k + 1] for k in range(K)]
    total = scores[0]
    for k in range(1, K):
        total = total + scores[k]
    hit = [(m[:, k : k + 1] == wanted).astype(f32) for k in range(K)]
    match = hit[0]
    weight = hit[0] * (route_scale * scores[0] / total)
    for k in range(1, K):
        match = match + hit[k]
        weight = weight + hit[k] * (route_scale * scores[k] / total)
    below = (
        lax.broadcasted_iota(jnp.int32, (NT, NT), 1) < lax.broadcasted_iota(jnp.int32, (NT, NT), 0)
    ).astype(bf16)
    rank = nn(below, match.astype(bf16))
    pick = jnp.where(rank == slot, match, 0.0)
    place = pick.astype(bf16)
    weight = weight * pick
    w_hi = weight.astype(bf16)
    w_lo = (weight - w_hi.astype(f32)).astype(bf16)

    xs = ((zg, sg, ag), (zu, su, au))

    def dispatch(a):
        z, s_, r_ = xs[a]

        def chunk(n):
            cols = pl.ds(pl.multiple_of(n * CD, CD), CD)
            s_[:, :, cols] = tn(place, z[:, :, cols].reshape(NT, CD)).astype(bf16).reshape(C, SL, CD)

            def send(off):
                p = lax.rem(c + off, C)
                remote(
                    s_.at[p, :, cols], r_.at[c, :, cols], x_ss.at[a * ND + n, p], x_rs.at[a * ND + n, c], {"ctx": p}
                ).start()

            each_peer(C, send)
            r_[c, :, cols] = s_[c, :, cols]

        each(0, ND, chunk)

    def arrived(a, n):
        z, s_, r_ = xs[a]
        cols = pl.ds(pl.multiple_of(n * CD, CD), CD)

        def one(off):
            p = lax.rem(c + C - off, C)
            remote(
                s_.at[p, :, cols], r_.at[p, :, cols], x_ss.at[a * ND + n, p], x_rs.at[a * ND + n, p], {"ctx": p}
            ).wait_recv()

        each_peer(C, one)
        return cols

    z_wait(1)
    dispatch(0)
    z_wait(2)
    dispatch(1)

    loads[0].wait()
    loads[1].wait()
    act[2] = jnp.zeros((NS, HID), f32)

    def d_hidden(n):
        cols = arrived(0, n)
        act[2] += nt(ag[:, :, cols].reshape(NS, CD), ds_[:, cols])

    each(0, ND, d_hidden)
    for i in range(2, 6):
        loads[i].wait()
    act[0] = jnp.zeros((NS, HID), f32)
    act[1] = jnp.zeros((NS, HID), f32)

    def gate_up(n):
        cols = arrived(1, n)
        x = au[:, :, cols].reshape(NS, CD)
        act[0] += nn(x, gs[cols, :])
        act[1] += nn(x, us[cols, :])

    each(0, ND, gate_up)
    a_, b_, dh = act[0], act[1], act[2]
    sig = jax.nn.sigmoid(a_)
    gated = a_ * sig
    hidden = (gated * b_).astype(bf16)
    d_gate = (dh * b_ * (sig * (1.0 + a_ * (1.0 - sig)))).astype(bf16)
    d_up = (dh * gated).astype(bf16)

    backs = ((ro, bo), (rd, bd))

    def send_back(a, n, cols):
        s_, r_ = backs[a]

        def send(off):
            p = lax.rem(c + off, C)
            remote(
                s_.at[p, :, cols], r_.at[c, :, cols], b_ss.at[a * NR + n, p], b_rs.at[a * NR + n, c], {"ctx": p}
            ).start()

        each_peer(C, send)
        r_[c, :, cols] = s_[c, :, cols]

    def result(n, wg):
        cols = pl.ds(pl.multiple_of(n * CR, CR), CR)
        y = nn(hidden, ds_[:, cols]).astype(bf16)
        ro[:, :, cols] = y.reshape(C, SL, CR)
        send_back(0, n, cols)
        return wg + jnp.sum(y.astype(f32) * ag[:, :, cols].reshape(NS, CR).astype(f32), axis=1, keepdims=True)

    wg = lax.fori_loop(0, NR, result, jnp.zeros((NS, 1), f32))
    rw[...] = jnp.broadcast_to(wg, (NS, rw.shape[2])).reshape(rw.shape)

    def send_w(off):
        p = lax.rem(c + off, C)
        remote(rw.at[p], bw.at[c], bw_ss.at[p], bw_rs.at[c], {"ctx": p}).start()

    each_peer(C, send_w)
    bw[c] = rw[c]

    def grads(n):
        cols = pl.ds(pl.multiple_of(n * CR, CR), CR)
        y = nt(d_gate, gs[cols, :]) + nt(d_up, us[cols, :])
        rd[:, :, cols] = y.astype(bf16).reshape(C, SL, CR)
        send_back(1, n, cols)

    each(0, NR, grads)

    sums = ((po, fo), (pd, fd))

    def combine(a):
        s_, r_ = backs[a]
        q_, e_ = sums[a]

        def chunk(n):
            cols = pl.ds(pl.multiple_of(n * CR, CR), CR)

            def one(off):
                p = lax.rem(c + C - off, C)
                remote(
                    s_.at[p, :, cols], r_.at[p, :, cols], b_ss.at[a * NR + n, p], b_rs.at[a * NR + n, p], {"ctx": p}
                ).wait_recv()

            each_peer(C, one)
            x = r_[:, :, cols].reshape(NS, CR)
            q_[:, :, cols] = (nn(w_hi, x) + nn(w_lo, x)).astype(bf16).reshape(T, tok, CR)

            def send(off):
                p = lax.rem(t + off, T)
                remote(
                    q_.at[p, :, cols], e_.at[t, :, cols], y_ss.at[a * NR + n, p], y_rs.at[a * NR + n, t], {"tp": p}
                ).start()

            each_peer(T, send)
            e_[t, :, cols] = q_[t, :, cols]

        each(0, NR, chunk)

    combine(0)

    def got_w(off):
        p = lax.rem(c + C - off, C)
        remote(rw.at[p], bw.at[p], bw_ss.at[p], bw_rs.at[p], {"ctx": p}).wait_recv()

    each_peer(C, got_w)
    wcol = bw[...].reshape(NS, bw.shape[2])
    wlane = lax.broadcasted_iota(jnp.int32, (NT, bw.shape[2]), 1)
    wgk = jnp.zeros((NT, bw.shape[2]), f32)
    for k in range(K):
        v = lax.dot_general(
            hit[k] * pick, wcol, (((1,), (0,)), ((), ())),
            preferred_element_type=f32, precision=lax.Precision.HIGHEST,
        )
        wgk = jnp.where(wlane == k, v, wgk)
    pw[...] = wgk.reshape(pw.shape)

    def send_pw(off):
        p = lax.rem(t + off, T)
        remote(pw.at[p], fw.at[t], yw_ss.at[p], yw_rs.at[t], {"tp": p}).start()

    each_peer(T, send_pw)
    fw[t] = pw[t]

    combine(1)

    def got(a):
        q_, e_ = sums[a]

        def chunk(n):
            cols = pl.ds(pl.multiple_of(n * CR, CR), CR)

            def one(off):
                p = lax.rem(t + T - off, T)
                remote(
                    q_.at[p, :, cols], e_.at[p, :, cols], y_ss.at[a * NR + n, p], y_rs.at[a * NR + n, p], {"tp": p}
                ).wait_recv()

            each_peer(T, one)

        each(0, NR, chunk)

    def total_of(e_):
        v = e_[0].astype(f32)
        for i in range(1, T):
            v = v + e_[i].astype(f32)
        return v

    h = hs[...]
    got(0)
    lo_o[...] = (h + total_of(fo)).astype(bf16)

    def got_pw(off):
        p = lax.rem(t + T - off, T)
        remote(pw.at[p], fw.at[p], yw_ss.at[p], yw_rs.at[p], {"tp": p}).wait_recv()

    each_peer(T, got_pw)
    wgt = total_of(fw)[:, 0:K]
    sc = meta[:, K : 2 * K]
    st = jnp.sum(sc, axis=1, keepdims=True)
    sg_o[...] = route_scale / st * (wgt - jnp.sum(wgt * sc, axis=1, keepdims=True) / st)

    got(1)
    dn = total_of(fd) * gain[...]
    inv = lax.rsqrt(jnp.mean(h * h, axis=1, keepdims=True) + norm_eps)
    proj = jnp.mean(dn * h, axis=1, keepdims=True)
    rg_o[...] = (g[...].astype(f32) + inv * dn - h * (inv * inv * inv * proj)).astype(bf16)

    for i, z in enumerate(zs):
        each_peer(
            T,
            lambda o: remote(
                z.at[t], z.at[t], z_ss.at[i, lax.rem(t + o, T)], z_rs.at[i, t], {"tp": lax.rem(t + o, T)}
            ).wait_send(),
        )

    def drain_x(off):
        p = lax.rem(c + off, C)
        remote(rw.at[p], bw.at[c], bw_ss.at[p], bw_rs.at[c], {"ctx": p}).wait_send()
        for a in range(2):
            def disp(n):
                cols = pl.ds(pl.multiple_of(n * CD, CD), CD)
                remote(
                    xs[a][1].at[p, :, cols], xs[a][2].at[c, :, cols], x_ss.at[a * ND + n, p], x_rs.at[a * ND + n, c],
                    {"ctx": p},
                ).wait_send()

            each(0, ND, disp)

            def back(n):
                cols = pl.ds(pl.multiple_of(n * CR, CR), CR)
                remote(
                    backs[a][0].at[p, :, cols], backs[a][1].at[c, :, cols], b_ss.at[a * NR + n, p],
                    b_rs.at[a * NR + n, c], {"ctx": p},
                ).wait_send()

            each(0, NR, back)

    each_peer(C, drain_x)

    def drain_z(off):
        p = lax.rem(t + off, T)
        remote(pw.at[p], fw.at[t], yw_ss.at[p], yw_rs.at[t], {"tp": p}).wait_send()
        for a in range(2):
            def back(n):
                cols = pl.ds(pl.multiple_of(n * CR, CR), CR)
                remote(
                    sums[a][0].at[p, :, cols], sums[a][1].at[t, :, cols], y_ss.at[a * NR + n, p],
                    y_rs.at[a * NR + n, t], {"tp": p},
                ).wait_send()

            each(0, NR, back)

    each_peer(T, drain_z)


VM = pl.BlockSpec(memory_space=pltpu.VMEM)
ANY = pl.BlockSpec(memory_space=pl.ANY)
LANES = 128


def per_device(
    C, T,
    query_latent, query_rotary, key_latent, key_rotary, value_up, out_proj, residual, norm_gain,
    gate_proj, up_proj, down_proj, expert_ids, route_score, out_grad,
):
    rows = query_latent.shape[1]
    H, LR, VD = value_up.shape
    LAT, ROPE = key_latent.shape[2], key_rotary.shape[2]
    KW = LAT + LANES
    tok, D = residual.shape[1:]
    OC = out_proj.shape[2]
    K = expert_ids.shape[2]
    DH, HID = gate_proj.shape[1:]
    HH = down_proj.shape[1]
    gain = norm_gain.reshape(1, D)
    gate_w, up_w, down_w = gate_proj[0], up_proj[0], down_proj[0]
    dma = pltpu.SemaphoreType.DMA
    shape = jax.ShapeDtypeStruct

    hs, normed, go, uo, do = pl.pallas_call(
        functools.partial(attn_kernel, C, T),
        name="attention",
        out_shape=(
            shape((tok, D), f32), shape((tok, D), bf16),
            shape((DH, HID), bf16), shape((DH, HID), bf16), shape((HH, D), bf16),
        ),
        in_specs=[VM] * 8 + [ANY] * 3,
        out_specs=(VM, VM, ANY, ANY, ANY),
        scratch_shapes=[
            pltpu.VMEM((H * rows, KW), bf16),
            pltpu.VMEM((C * rows, KW), bf16),
            pltpu.VMEM((2 * rows, C * rows), f32),
            pltpu.VMEM((H, LAT, VD), bf16),
            pltpu.VMEM((D, H * VD), bf16),
            pltpu.VMEM((H * rows, LAT), bf16),
            pltpu.VMEM((rows, H * VD), bf16),
            pltpu.VMEM((T, tok, D), bf16),
            pltpu.VMEM((T, tok, D), bf16),
            dma((3,)), dma((3,)),
        ] + [dma((C,))] * 10 + [dma((T,))] * 2,
        compiler_params=pltpu.CompilerParams(
            collective_id=0, has_side_effects=True, vmem_limit_bytes=56 * 1024 * 1024
        ),
    )(
        query_latent[0], query_rotary[0], key_latent[0], key_rotary[0], value_up, out_proj, residual[0], gain,
        gate_w, up_w, down_w,
    )

    meta = jnp.concatenate(
        [expert_ids[0].astype(f32), route_score[0], jnp.zeros((tok, LANES - 2 * K), f32)], axis=1
    )
    SL = CAP * T
    NS = C * SL
    ND, NR = 2, 4
    xy = (C, SL, D)
    zz = (T, tok, D)
    layer_out, resid_grad, score_grad = pl.pallas_call(
        functools.partial(moe_kernel, C, T, K, ND, NR),
        name="experts",
        out_shape=(shape((tok, D), bf16), shape((tok, D), bf16), shape((tok, K), f32)),
        in_specs=[VM] * 5 + [ANY] * 6,
        out_specs=(VM, VM, VM),
        scratch_shapes=[
            pltpu.VMEM((D, HID), bf16), pltpu.VMEM((D, HID), bf16), pltpu.VMEM((HID, D), bf16),
            pltpu.VMEM(zz, bf16), pltpu.VMEM(zz, bf16), pltpu.VMEM((T, tok, LANES), f32),
            pltpu.VMEM(xy, bf16), pltpu.VMEM(xy, bf16), pltpu.VMEM(xy, bf16), pltpu.VMEM(xy, bf16),
            pltpu.VMEM((3, NS, HID), f32),
            pltpu.VMEM(xy, bf16), pltpu.VMEM(xy, bf16), pltpu.VMEM((C, SL, LANES), f32),
            pltpu.VMEM(xy, bf16), pltpu.VMEM(xy, bf16), pltpu.VMEM((C, SL, LANES), f32),
            pltpu.VMEM(zz, bf16), pltpu.VMEM(zz, bf16), pltpu.VMEM((T, tok, LANES), f32),
            pltpu.VMEM(zz, bf16), pltpu.VMEM(zz, bf16), pltpu.VMEM((T, tok, LANES), f32),
            dma((3, 2)),
            dma((3, T)), dma((3, T)),
            dma((2 * ND, C)), dma((2 * ND, C)),
            dma((2 * NR, C)), dma((2 * NR, C)),
            dma((C,)), dma((C,)),
            dma((2 * NR, T)), dma((2 * NR, T)),
            dma((T,)), dma((T,)),
        ],
        compiler_params=pltpu.CompilerParams(
            collective_id=1, has_side_effects=True, vmem_limit_bytes=60 * 1024 * 1024
        ),
    )(normed, out_grad[0], meta, hs, gain, gate_w, up_w, down_w, go, uo, do)
    return (layer_out[None], resid_grad[None], score_grad[None])


def solution(mesh):
    return jax.shard_map(
        functools.partial(per_device, mesh.shape["ctx"], mesh.shape["tp"]),
        mesh=mesh,
        in_specs=(
            P("dp", "ctx", "tp"),
            P("dp", "ctx", "tp"),
            P("dp", "ctx", None),
            P("dp", "ctx", None),
            P("tp", "ctx", None),
            P("tp", None, "ctx"),
            P("dp", ("ctx", "tp"), None),
            P(),
            P(("ctx", "tp"), "dp", None),
            P(("ctx", "tp"), "dp", None),
            P(("ctx", "tp"), "dp", None),
            P("dp", ("ctx", "tp"), None),
            P("dp", ("ctx", "tp"), None),
            P("dp", ("ctx", "tp"), None),
        ),
        out_specs=(
            P("dp", ("ctx", "tp"), None),
            P("dp", ("ctx", "tp"), None),
            P("dp", ("ctx", "tp"), None),
        ),
        check_vma=False,
    )
```

time: 530 us -> 281 us (0.53); the launches traced: 522 us -> 281 us
  waiting for transfers between devices: 325 us -> 0 us
  Pallas kernels: 0 us -> 270 us
  matrix products: 67.2 us -> 0 us
  starting transfers between devices: 31.9 us -> 0 us
  local copies, waits for them, and re-layouts: 41.3 us -> 9.47 us
  blocking collectives: 24.5 us -> 0 us
  between operations: 16.1 us -> 0.67 us
  other arithmetic: 15.6 us -> 0.68 us
    pallas_call x0 -> x2, Pallas kernels: none -> 270 us  [the longest x1 142 us: per_device(): pl.pallas_call(functools.partial(moe_kernel, C, T, K, ND, NR), name='expe...]
    all_to_all x2 -> x0, waiting for transfers between devices: 163 us -> none  [the longest x1 82.3 us: per_device(): lax.all_to_all(outgoing, ('ctx', 'tp'), split_axis=0, concat_axis=0, tile...]
    all_gather x6 -> x0, waiting for transfers between devices: 135 us -> none  [the longest x1 73.1 us: per_device(): lax.all_gather(out_proj, 'ctx', axis=2, tiled=True)]
    dot_general x15 -> x0, matrix products: 67.2 us -> none  [the longest x1 7.28 us: expert_pass(): act_b = jnp.dot(rows_u, up_w, preferred_element_type=jnp.float32)]
    all_gather x1 -> x0, blocking collectives: 24.5 us -> none  [per_device(): lax.all_gather(key_rotary, 'ctx', axis=1, tiled=True)]
    reduce_scatter x1 -> x0, waiting for transfers between devices: 24.1 us -> none  [per_device(): lax.psum_scatter(jnp.dot(heads_out, flat_out, preferred_element_type=jnp....]
    all_to_all x2 -> x0, starting transfers between devices: 20 us -> none  [the longest x1 12.2 us: per_device(): lax.all_to_all(outgoing, ('ctx', 'tp'), split_axis=0, concat_axis=0, tile...]
    all_gather x6 -> x0, starting transfers between devices: 11.8 us -> none  [the longest x1 11.6 us: per_device(): lax.all_gather(up_proj, 'dp', axis=1, tiled=True)]
  transfers between devices with their start and end apart: 9 -> 0, of which waited for: 6 -> 0; matrix products, arithmetic and copies ran while one was open for 11% -> 0% of each run, Pallas kernels for 0% -> 0%
where the time goes in v1:
time: 281 us
  Pallas kernels  270 us (96%)
  local copies, waits for them, and re-layouts  9.47 us (3%)
    pallas_call x1, Pallas kernels, per_device(): pl.pallas_call(functools.partial(moe_kernel, C, T, K, ND, NR), name='expe...  142 us
    pallas_call x1, Pallas kernels, per_device(): pl.pallas_call(functools.partial(attn_kernel, C, T), name='attention', ou...  128 us
    unnamed x8, local copies, waits for them, and re-layouts  6.56 us

profile of v1, /device:TPU:32, one launch (start us, length us, event | category | flops | bytes accessed | tf_op | source)
XLA Modules:
  0.0 280.5 jit_solution(4330981593395012921)
XLA Ops:
  0.6 1.3 reshape.10.gain
  2.0 2.0 copy.18.os_
  4.0 1.4 copy.17
  5.4 0.0 copy-start.1
  5.4 0.0 copy-start
  5.4 127.8 %attention.1 = (f32[16,3584]{1,0:T(8,128)}, bf16[16,3584]{1,0:T(8,128)(2,1)}, bf16[1792,1024]{1,0:T(8,128)(2,1)}, bf16[1792,1024]{1,0:T(8,128)(2,1)}, bf16[512,3584]{1,0:T(8,128)(2,1)}) custom-call(bf16[128,4096]{1,0:T(8,128)(2,1)} %bitcast.21, bf16[128,512]{1,0:T(8,128)(2,1)} %bitcast.22, bf16[128,512]{1,0:T(8,128)(2,1)} %bitcast.23, ...), custom_call_target="tpu_custom_call" | custom-call | tf_op jit(solution)/shard_map/attention/pallas_call | solution.py:564
  133.2 0.0 copy-done.1
  133.2 0.1 copy.19
  133.3 0.0 copy-done
  133.3 0.1 copy.20
  133.4 0.1 pad.2.clone
  133.4 0.7 maximum_maximum_fusion.meta
  134.1 141.9 %experts.1 = (bf16[16,3584]{1,0:T(8,128)(2,1)}, bf16[16,3584]{1,0:T(8,128)(2,1)}, f32[16,8]{1,0:T(8,128)}) custom-call(bf16[16,3584]{1,0:T(8,128)(2,1)} %get-tuple-element.11.u, bf16[16,3584]{1,0:T(8,128)(2,1)} %bitcast.28, f32[16,128]{1,0:T(8,128)} %maximum_maximum_fusion.meta, f32[16,3584]{1,0:T(8,128)} %get-tuple-element.12.hs, f32[1,3584]{1,0:T(1,128)} %reshape.10.gain, ...), custom_call_target="tpu_custom_call" | custom-call | tf_op jit(solution)/shard_map/experts/pallas_call | solution.py:601
  276.1 1.4 copy.21
  277.4 1.6 copy.24
  279.0 1.6 copy.25
  (2 shorter events, 0.0 us)
Async XLA Ops:
  5.4 127.8 %copy-start.1 = (s32[1,16,8]{1,2,0:T(8,128)S(1)}, s32[1,16,8]{1,2,0:T(8,128)}, u32[]{:S(2)}) copy-start(s32[1,16,8]{1,2,0:T(8,128)} %param.25) | copy-start | bytes 1540
  5.4 127.9 %copy-start = (f32[1,16,8]{1,2,0:T(8,128)S(1)}, f32[1,16,8]{1,2,0:T(8,128)}, u32[]{:S(2)}) copy-start(f32[1,16,8]{1,2,0:T(8,128)} %param.26) | copy-start | bytes 1540

commit v2 on v0

v2 whole, which is shorter than its diff:
```python
import functools
import math

import jax
import jax.numpy as jnp
from jax import lax
from jax.experimental import pallas as pl
from jax.experimental.pallas import tpu as pltpu
from jax.sharding import PartitionSpec as P

MESH = pl.DeviceIdType.MESH
f32 = jnp.float32
bf16 = jnp.bfloat16
route_scale = 2.5
norm_eps = 1e-06
CAP = 2
LANES = 128


def remote(src, dst, send_sem, recv_sem, device):
    return pltpu.make_async_remote_copy(
        src_ref=src, dst_ref=dst, send_sem=send_sem, recv_sem=recv_sem, device_id=device, device_id_type=MESH
    )


def each(lo, hi, fn):
    def body(i, carry):
        fn(i)
        return carry

    lax.fori_loop(lo, hi, body, 0)


def nt(a, b):
    return lax.dot_general(a, b, (((1,), (1,)), ((), ())), preferred_element_type=f32)


def nn(a, b):
    return lax.dot_general(a, b, (((1,), (0,)), ((), ())), preferred_element_type=f32)


def tn(a, b):
    return lax.dot_general(a, b, (((0,), (0,)), ((), ())), preferred_element_type=f32)


def identity(n):
    return (lax.broadcasted_iota(jnp.int32, (n, n), 0) == lax.broadcasted_iota(jnp.int32, (n, n), 1)).astype(bf16)


def row_of(ref):
    return jnp.concatenate([ref[i : i + 1, :] for i in range(ref.shape[0])], axis=1)


def tour(n):
    if n == 4:
        return [(1, 0), (0, 1), (3, 0), (0, 3), (1, 1), (3, 3), (1, 3), (3, 1), (2, 0), (0, 2), (2, 1), (1, 2),
                (2, 3), (3, 2), (2, 2)]
    return [(i % n, i // n) for i in range(1, n * n)]


def main_kernel(
    C, T, K, ND, NR,
    ql, qr, kl, krt, vs, ost, res, gain, g, meta, gw, uw, dw,
    hs_o, so_o, dn_o, wg_o,
    qbuf, kbuf, vbuf, obuf, us, ds_, heads, part, rsb, zm, zg, zu, sx, ag, au, act, ab, place, wts,
    ro, rd, rw, bo, bd, bw, pd, pw, fo, fd, fw,
    wl, w_ss, w_rs, k_ss, k_rs, v_ss, v_rs, o_ss, o_rs, sv_ss, sv_rs, so_ss, so_rs, r_ss, r_rs,
    zm_ss, zm_rs, zg_ss, zg_rs, zu_ss, zu_rs, xg_ss, xg_rs, xu_ss, xu_rs, b_ss, b_rs, bw_ss, bw_rs,
    y_ss, y_rs, yw_ss, yw_rs, ready,
):
    c, t, d = lax.axis_index("ctx"), lax.axis_index("tp"), lax.axis_index("dp")
    NX = math.isqrt(C)
    rows = ql.shape[0]
    H, LR, VD = vs.shape
    LAT = kl.shape[1]
    ROPE = krt.shape[0]
    KW = kbuf.shape[1]
    OC = ost.shape[1]
    OH = OC // 2
    Hh = H // 2
    tok, D = res.shape
    DH, HH = gw.shape[0], dw.shape[0]
    HID = 2 * HH
    SL = CAP * T
    NT = T * tok
    NS = C * SL
    CD, CG, CR = D // ND, D // 2, D // NR
    scale = (VD + ROPE) ** (-0.5)
    sib = {"dp": 1 - d}
    gs = obuf

    row, col = lax.div(c, NX), lax.rem(c, NX)
    a = col * (1 - d) + row * d
    b = row * (1 - d) + col * d
    sa, sb = 1 + (NX - 1) * d, NX - (NX - 1) * d

    def at(da, db):
        return lax.rem(a + da, NX) * sa + lax.rem(b + db, NX) * sb

    hops = tour(NX)

    def to_xy(fn):
        for da, db in hops:
            fn(at(da, db))

    def from_xy(fn):
        each(1, C, lambda off: fn(lax.rem(c + C - off, C)))

    def to_z(fn):
        each(1, T, lambda off: fn(lax.rem(t + off, T)))

    def from_z(fn):
        each(1, T, lambda off: fn(lax.rem(t + T - off, T)))

    bar = pltpu.get_barrier_semaphore()
    from_xy(lambda p: pl.semaphore_signal(bar, inc=1, device_id={"ctx": p}, device_id_type=MESH))
    to_z(lambda p: pl.semaphore_signal(bar, inc=1, device_id={"tp": p}, device_id_type=MESH))
    pl.semaphore_signal(bar, inc=1, device_id=sib, device_id_type=MESH)

    def half_rows(ref, who, n):
        return ref.at[pl.ds(pl.multiple_of(who * n, n), n)]

    own_d = pltpu.make_async_copy(dw, half_rows(ds_, d, HH), wl.at[0])
    own_u = pltpu.make_async_copy(uw, half_rows(us, d, DH), wl.at[1])
    own_g = pltpu.make_async_copy(gw, half_rows(gs, d, DH), wl.at[2])
    own_d.start()
    own_u.start()
    swap_d = remote(dw, half_rows(ds_, d, HH), w_ss.at[0], w_rs.at[0], sib)
    swap_u = remote(uw, half_rows(us, d, DH), w_ss.at[1], w_rs.at[1], sib)
    swap_g = remote(gw, half_rows(gs, d, DH), w_ss.at[2], w_rs.at[2], sib)

    def key_rows(i):
        return kbuf.at[pl.ds(pl.multiple_of(i * rows, rows), rows)]

    my_keys = pl.ds(pl.multiple_of(c * rows, rows), rows)
    kbuf[my_keys, 0:LAT] = kl[...]
    kr = tn(krt[...], identity(ROPE)).astype(bf16)
    kbuf[my_keys, LAT:KW] = jnp.concatenate([kr, jnp.zeros((rows, KW - LAT - ROPE), bf16)], axis=1)
    zm[t] = meta[...]
    zg[t] = g[...]
    pl.semaphore_wait(bar, C + T - 1)

    def send_keys(p):
        @pl.when(p > c)
        def _():
            remote(key_rows(c), key_rows(c), k_ss.at[p], k_rs.at[c], {"ctx": p}).start()

    to_xy(send_keys)
    to_z(lambda p: remote(zm.at[t], zm.at[t], zm_ss.at[p], zm_rs.at[t], {"tp": p}).start())
    to_z(lambda p: remote(zg.at[t], zg.at[t], zg_ss.at[p], zg_rs.at[t], {"tp": p}).start())
    swap_d.start()
    swap_u.start()

    for h in range(H):
        obuf[pl.ds(pl.multiple_of(c * OC, OC), OC), h * VD : (h + 1) * VD] = ost[h]
    vbuf[:, pl.ds(pl.multiple_of(c * LR, LR), LR), :] = vs[...]

    def v_part(owner, half):
        return vbuf.at[pl.ds(half * Hh, Hh), pl.ds(pl.multiple_of(owner * LR, LR), LR), :]

    def o_part(owner, half):
        return obuf.at[pl.ds(pl.multiple_of(owner * OC + half * OH, OH), OH), :]

    def vo(owner, s, dest):
        return (
            remote(o_part(owner, d), o_part(owner, d), o_ss.at[s], o_rs.at[owner], {"ctx": dest}),
            remote(v_part(owner, d), v_part(owner, d), v_ss.at[s], v_rs.at[owner], {"ctx": dest}),
        )

    def vo_relay(owner, half):
        return (
            remote(o_part(owner, half), o_part(owner, half), so_ss.at[owner], so_rs.at[owner], sib),
            remote(v_part(owner, half), v_part(owner, half), sv_ss.at[owner], sv_rs.at[owner], sib),
        )

    def start(copies):
        for x in copies:
            x.start()

    def wait_recv(copies):
        for x in copies:
            x.wait_recv()

    def wait_send(copies):
        for x in copies:
            x.wait_send()

    def blank(j):
        kbuf[pl.ds(pl.multiple_of(j * rows, rows), rows), :] = jnp.zeros((rows, KW), bf16)

    each(c + 1, C, blank)
    for h in range(H):
        qbuf[h * rows : (h + 1) * rows, 0:LAT] = ql[:, h * LAT : (h + 1) * LAT]
        qbuf[h * rows : (h + 1) * rows, LAT:KW] = jnp.concatenate(
            [qr[:, h * ROPE : (h + 1) * ROPE], jnp.zeros((rows, KW - LAT - ROPE), bf16)], axis=1
        )

    each(0, c, lambda j: remote(key_rows(j), key_rows(j), k_ss.at[j], k_rs.at[j], {"ctx": j}).wait_recv())

    for o in range(1, NX):
        start(vo(c, o, at(o, 0)))
    for o in range(1, NX):
        start(vo(c, NX + o, at(0, o)))

    def pass_on(i):
        owner = lax.rem(a + NX - i, NX) * sa + b * sb
        wait_recv(vo(owner, 0, owner))
        for o in range(1, NX):
            start(vo(owner, NX * (i + 1) + o, at(0, o)))
        start(vo_relay(owner, d))

    S = C * rows
    NB = 4
    SN = S // NB
    MB = 2 * rows

    def sc(n):
        return act.at[n // 2, 0:MB, (n % 2) * SN : (n % 2 + 1) * SN]

    def attend(i):
        @pl.when(jnp.logical_and(i > 0, i < NX))
        def _():
            pass_on(i)

        r = pl.ds(pl.multiple_of(i * MB, MB), MB)
        q = qbuf[r, :]
        qpos = c * rows + lax.rem(lax.broadcasted_iota(jnp.int32, (MB, SN), 0), rows)
        kpos = lax.broadcasted_iota(jnp.int32, (MB, SN), 1)
        top = jnp.full((MB, 1), -1e30, f32)
        for n in range(NB):
            s = nt(q, kbuf[n * SN : (n + 1) * SN, :]) * scale
            s = jnp.where(kpos + n * SN <= qpos, s, -1e30)
            sc(n)[...] = s
            top = jnp.maximum(top, jnp.max(s, axis=1, keepdims=True))
        total = jnp.zeros((MB, 1), f32)
        acc = jnp.zeros((MB, LAT), f32)
        for n in range(NB):
            p = jnp.exp(sc(n)[...] - top)
            total = total + jnp.sum(p, axis=1, keepdims=True)
            acc = acc + nn(p.astype(bf16), kbuf[n * SN : (n + 1) * SN, 0:LAT])
        qbuf[r, 0:LAT] = (acc / total).astype(bf16)

    each(0, H // 2, attend)

    from_z(lambda p: remote(zm.at[p], zm.at[p], zm_ss.at[p], zm_rs.at[p], {"tp": p}).wait_recv())
    lane = lax.broadcasted_iota(jnp.int32, (NT, NS), 1)
    wanted = (lax.div(lane, SL) * T + t).astype(f32)

    def hit(k):
        return (zm[...].reshape(NT, LANES)[:, k : k + 1] == wanted).astype(f32)

    m = zm[...].reshape(NT, LANES)
    total = m[:, K : K + 1]
    for k in range(1, K):
        total = total + m[:, K + k : K + k + 1]
    match = hit(0)
    weight = match * (route_scale * m[:, K : K + 1] / total)
    for k in range(1, K):
        h_ = hit(k)
        match = match + h_
        weight = weight + h_ * (route_scale * m[:, K + k : K + k + 1] / total)
    below = (
        lax.broadcasted_iota(jnp.int32, (NT, NT), 1) < lax.broadcasted_iota(jnp.int32, (NT, NT), 0)
    ).astype(bf16)
    rank = nn(below, match.astype(bf16))
    pick = jnp.where(rank == lax.rem(lane, SL).astype(f32), match, 0.0)
    place[...] = pick.astype(bf16)
    weight = weight * pick
    w_hi = weight.astype(bf16)
    wts[0] = w_hi
    wts[1] = (weight - w_hi.astype(f32)).astype(bf16)

    from_z(lambda p: remote(zg.at[p], zg.at[p], zg_ss.at[p], zg_rs.at[p], {"tp": p}).wait_recv())

    def g_cols(n):
        return pl.ds(pl.multiple_of(n * CG, CG), CG)

    def place_g(n):
        cols = g_cols(n)
        sx[:, :, cols] = tn(place[...], zg[:, :, cols].reshape(NT, CG)).astype(bf16).reshape(C, SL, CG)
        ag[c, :, cols] = sx[c, :, cols]

    each(0, 2, place_g)

    def relay(bo_):
        def one(ai):
            owner = lax.rem(a + ai, NX) * sa + lax.rem(b + NX - bo_, NX) * sb
            wait_recv(vo(owner, 0, owner))
            start(vo_relay(owner, d))

        each(0, NX, one)

    for o in (1, 3, 2) if NX == 4 else range(1, NX):
        relay(o)

    def xg(n, p, q):
        cols = g_cols(n)
        return remote(sx.at[p, :, cols], ag.at[q, :, cols], xg_ss.at[n, p], xg_rs.at[n, q], {"ctx": p})

    each(0, 2, lambda n: to_xy(lambda p: xg(n, p, c).start()))

    from_xy(lambda p: wait_recv(vo_relay(p, 1 - d)))

    for h in range(H):
        heads[:, h * VD : (h + 1) * VD] = nn(qbuf[h * rows : (h + 1) * rows, 0:LAT], vbuf[h]).astype(bf16)

    PN = 512 if D % 512 == 0 else D

    def project(n):
        cols = pl.ds(pl.multiple_of(n * PN, PN), PN)
        part[:, :, cols] = nt(heads[...], obuf[cols, :]).astype(bf16).reshape(T, tok, PN)

    each(0, D // PN, project)
    to_z(lambda p: remote(part.at[p], rsb.at[t], r_ss.at[p], r_rs.at[t], {"tp": p}).start())
    rsb[t] = part[t]

    def sent_vo(off):
        for o in range(1, NX):
            wait_send(vo(c, NX * off + o, c))

    each(0, NX + 1, sent_vo)
    from_xy(lambda p: wait_send(vo_relay(p, d)))
    pl.semaphore_signal(ready, inc=1, device_id=sib, device_id_type=MESH)
    own_g.start()

    from_z(lambda p: remote(part.at[p], rsb.at[p], r_ss.at[p], r_rs.at[p], {"tp": p}).wait_recv())
    hs = rsb[0].astype(f32)
    for i in range(1, T):
        hs = hs + rsb[i].astype(f32)
    hs = hs + res[...].astype(f32)
    hs_o[...] = hs
    inv = lax.rsqrt(jnp.mean(hs * hs, axis=1, keepdims=True) + norm_eps)
    zu[t] = (hs * inv * row_of(gain)).astype(bf16)

    def u_cols(n):
        return pl.ds(pl.multiple_of(n * CD, CD), CD)

    def z_u(n, p, q):
        cols = u_cols(n)
        return remote(zu.at[q, :, cols], zu.at[q, :, cols], zu_ss.at[n, p], zu_rs.at[n, q], {"tp": p})

    each(0, ND, lambda n: to_z(lambda p: z_u(n, p, t).start()))
    pl.semaphore_wait(ready, 1)
    swap_g.start()
    each(0, 2, lambda n: from_xy(lambda p: xg(n, p, c).wait_send()))

    def x_u(n, p, q):
        cols = u_cols(n)
        return remote(sx.at[p, :, cols], au.at[q, :, cols], xu_ss.at[n, p], xu_rs.at[n, q], {"ctx": p})

    def send_u(n):
        cols = u_cols(n)
        from_z(lambda p: z_u(n, p, p).wait_recv())
        sx[:, :, cols] = tn(place[...], zu[:, :, cols].reshape(NT, CD)).astype(bf16).reshape(C, SL, CD)
        to_xy(lambda p: x_u(n, p, c).start())
        au[c, :, cols] = sx[c, :, cols]

    each(0, ND, send_u)

    own_d.wait()
    swap_d.wait()
    act[2] = jnp.zeros((NS, HID), f32)

    def d_hidden(n):
        from_xy(lambda p: xg(n, p, p).wait_recv())
        cols = g_cols(n)
        act[2] += nt(ag[:, :, cols].reshape(NS, CG), ds_[:, cols])

    each(0, 2, d_hidden)
    own_u.wait()
    swap_u.wait()
    own_g.wait()
    swap_g.wait()
    act[0] = jnp.zeros((NS, HID), f32)
    act[1] = jnp.zeros((NS, HID), f32)

    def gate_up(n):
        from_xy(lambda p: x_u(n, p, p).wait_recv())
        cols = u_cols(n)
        x = au[:, :, cols].reshape(NS, CD)
        act[0] += nn(x, gs[cols, :])
        act[1] += nn(x, us[cols, :])

    each(0, ND, gate_up)

    EB = NS // 4

    def pointwise(i):
        r = pl.ds(pl.multiple_of(i * EB, EB), EB)
        a_, b_, dh = act[0, r, :], act[1, r, :], act[2, r, :]
        sig = jax.nn.sigmoid(a_)
        gated = a_ * sig
        ab[0, r, :] = (gated * b_).astype(bf16)
        ab[1, r, :] = (dh * b_ * (sig * (1.0 + a_ * (1.0 - sig)))).astype(bf16)
        ab[2, r, :] = (dh * gated).astype(bf16)

    each(0, 4, pointwise)

    backs = ((ro, bo), (rd, bd))

    def r_cols(n):
        return pl.ds(pl.multiple_of(n * CR, CR), CR)

    def back(i, n, p, q):
        s_, r_ = backs[i]
        cols = r_cols(n)
        return remote(s_.at[p, :, cols], r_.at[q, :, cols], b_ss.at[i * NR + n, p], b_rs.at[i * NR + n, q], {"ctx": p})

    def w_back(p, q):
        return remote(rw.at[p], bw.at[q], bw_ss.at[p], bw_rs.at[q], {"ctx": p})

    def result(n, wg):
        cols = r_cols(n)
        y = nn(ab[0], ds_[:, cols]).astype(bf16)
        ro[:, :, cols] = y.reshape(C, SL, CR)
        to_xy(lambda p: back(0, n, p, c).start())
        bo[c, :, cols] = ro[c, :, cols]
        return wg + jnp.sum(y.astype(f32) * ag[:, :, cols].reshape(NS, CR).astype(f32), axis=1, keepdims=True)

    wg = lax.fori_loop(0, NR, result, jnp.zeros((NS, 1), f32))
    rw[...] = jnp.broadcast_to(wg, (NS, LANES)).reshape(rw.shape)
    to_xy(lambda p: w_back(p, c).start())
    bw[c] = rw[c]

    def grads(n):
        cols = r_cols(n)
        y = nt(ab[1], gs[cols, :]) + nt(ab[2], us[cols, :])
        rd[:, :, cols] = y.astype(bf16).reshape(C, SL, CR)
        to_xy(lambda p: back(1, n, p, c).start())
        bd[c, :, cols] = rd[c, :, cols]

    each(0, NR, grads)

    to_z(lambda p: remote(part.at[p], rsb.at[t], r_ss.at[p], r_rs.at[t], {"tp": p}).wait_send())
    sums = ((part, fo), (pd, fd))

    def z_back(i, n, p, q):
        s_, r_ = sums[i]
        cols = r_cols(n)
        return remote(s_.at[p, :, cols], r_.at[q, :, cols], y_ss.at[i * NR + n, p], y_rs.at[i * NR + n, q], {"tp": p})

    def w_sum(p, q):
        return remote(pw.at[p], fw.at[q], yw_ss.at[p], yw_rs.at[q], {"tp": p})

    def combine(i):
        def chunk(n):
            cols = r_cols(n)
            from_xy(lambda p: back(i, n, p, p).wait_recv())
            x = backs[i][1][:, :, cols].reshape(NS, CR)
            sums[i][0][:, :, cols] = (nn(wts[0], x) + nn(wts[1], x)).astype(bf16).reshape(T, tok, CR)
            to_z(lambda p: z_back(i, n, p, t).start())
            sums[i][1][t, :, cols] = sums[i][0][t, :, cols]

        each(0, NR, chunk)

    combine(0)
    from_xy(lambda p: w_back(p, p).wait_recv())
    wcol = bw[...].reshape(NS, LANES)
    wlane = lax.broadcasted_iota(jnp.int32, (NT, LANES), 1)
    wgk = jnp.zeros((NT, LANES), f32)
    chosen = place[...].astype(f32)
    for k in range(K):
        v = lax.dot_general(
            hit(k) * chosen, wcol, (((1,), (0,)), ((), ())), preferred_element_type=f32, precision=lax.Precision.HIGHEST
        )
        wgk = jnp.where(wlane == k, v, wgk)
    pw[...] = wgk.reshape(pw.shape)
    to_z(lambda p: w_sum(p, t).start())
    fw[t] = pw[t]
    combine(1)

    def total_of(ref):
        v = ref[0].astype(f32)
        for i in range(1, T):
            v = v + ref[i].astype(f32)
        return v

    each(0, NR, lambda n: from_z(lambda p: z_back(0, n, p, p).wait_recv()))
    so_o[...] = total_of(fo)
    from_z(lambda p: w_sum(p, p).wait_recv())
    wg_o[...] = total_of(fw)

    to_z(lambda p: remote(zm.at[t], zm.at[t], zm_ss.at[p], zm_rs.at[t], {"tp": p}).wait_send())
    to_z(lambda p: remote(zg.at[t], zg.at[t], zg_ss.at[p], zg_rs.at[t], {"tp": p}).wait_send())
    each(0, ND, lambda n: to_z(lambda p: z_u(n, p, t).wait_send()))
    each(0, ND, lambda n: from_xy(lambda p: x_u(n, p, c).wait_send()))
    for i in range(2):
        each(0, NR, lambda n: from_xy(lambda p: back(i, n, p, c).wait_send()))
    from_xy(lambda p: w_back(p, c).wait_send())
    each(c + 1, C, lambda j: remote(key_rows(c), key_rows(c), k_ss.at[j], k_rs.at[c], {"ctx": j}).wait_send())

    each(0, NR, lambda n: from_z(lambda p: z_back(1, n, p, p).wait_recv()))
    dn_o[...] = total_of(fd)
    to_z(lambda p: w_sum(p, t).wait_send())
    for i in range(2):
        each(0, NR, lambda n: to_z(lambda p: z_back(i, n, p, t).wait_send()))


def final_kernel(K, hs, so, dn, wg, g, meta, gain, lo_o, rg_o, sg_o):
    h = hs[...]
    lo_o[...] = (h + so[...]).astype(bf16)
    wgt = wg[:, 0:K]
    sc = meta[:, K : 2 * K]
    st = jnp.sum(sc, axis=1, keepdims=True)
    sg_o[...] = route_scale / st * (wgt - jnp.sum(wgt * sc, axis=1, keepdims=True) / st)
    dng = dn[...] * row_of(gain)
    inv = lax.rsqrt(jnp.mean(h * h, axis=1, keepdims=True) + norm_eps)
    proj = jnp.mean(dng * h, axis=1, keepdims=True)
    rg_o[...] = (g[...].astype(f32) + inv * dng - h * (inv * inv * inv * proj)).astype(bf16)


VM = pl.BlockSpec(memory_space=pltpu.VMEM)
ANY = pl.BlockSpec(memory_space=pl.ANY)


def per_device(
    C, T,
    query_latent, query_rotary, key_latent, key_rotary, value_up, out_proj, residual, norm_gain,
    gate_proj, up_proj, down_proj, expert_ids, route_score, out_grad,
):
    rows = query_latent.shape[1]
    H, LR, VD = value_up.shape
    LAT, ROPE = key_latent.shape[2], key_rotary.shape[2]
    KW = LAT + LANES
    tok, D = residual.shape[1:]
    K = expert_ids.shape[2]
    HID = gate_proj.shape[2]
    SL = CAP * T
    NS = C * SL
    NT = T * tok
    NX = math.isqrt(C)
    ND, NR = 4, 4
    gain = norm_gain.reshape(D // LANES, LANES)
    meta = jnp.concatenate(
        [expert_ids[0].astype(f32), route_score[0], jnp.zeros((tok, LANES - 2 * K), f32)], axis=1
    )
    dma = pltpu.SemaphoreType.DMA
    shape = jax.ShapeDtypeStruct
    vmem = pltpu.VMEM
    xy = (C, SL, D)
    zz = (T, tok, D)

    hs, so, dn, wg = pl.pallas_call(
        functools.partial(main_kernel, C, T, K, ND, NR),
        name="layer",
        out_shape=(shape((tok, D), f32), shape((tok, D), f32), shape((tok, D), f32), shape((tok, LANES), f32)),
        in_specs=[VM] * 10 + [ANY] * 3,
        out_specs=(VM,) * 4,
        scratch_shapes=[
            vmem((H * rows, KW), bf16),
            vmem((C * rows, KW), bf16),
            vmem((H, LAT, VD), bf16),
            vmem((D, H * VD), bf16),
            vmem((D, HID), bf16),
            vmem((HID, D), bf16),
            vmem((rows, H * VD), bf16),
            vmem(zz, bf16), vmem(zz, bf16),
            vmem((T, tok, LANES), f32), vmem(zz, bf16), vmem(zz, bf16),
            vmem(xy, bf16), vmem(xy, bf16), vmem(xy, bf16),
            vmem((3, NS, HID), f32),
            vmem((3, NS, HID), bf16),
            vmem((NT, NS), bf16), vmem((2, NT, NS), bf16),
            vmem(xy, bf16), vmem(xy, bf16), vmem((C, SL, LANES), f32),
            vmem(xy, bf16), vmem(xy, bf16), vmem((C, SL, LANES), f32),
            vmem(zz, bf16), vmem((T, tok, LANES), f32),
            vmem(zz, bf16), vmem(zz, bf16), vmem((T, tok, LANES), f32),
            dma((3,)), dma((3,)), dma((3,)),
            dma((C,)), dma((C,)),
            dma((NX * (NX + 1),)), dma((C,)), dma((NX * (NX + 1),)), dma((C,)),
            dma((C,)), dma((C,)), dma((C,)), dma((C,)),
            dma((T,)), dma((T,)),
            dma((T,)), dma((T,)), dma((T,)), dma((T,)), dma((ND, T)), dma((ND, T)),
            dma((2, C)), dma((2, C)), dma((ND, C)), dma((ND, C)),
            dma((2 * NR, C)), dma((2 * NR, C)), dma((C,)), dma((C,)),
            dma((2 * NR, T)), dma((2 * NR, T)), dma((T,)), dma((T,)),
            pltpu.SemaphoreType.REGULAR,
        ],
        compiler_params=pltpu.CompilerParams(
            collective_id=0, has_side_effects=True, vmem_limit_bytes=60 * 1024 * 1024
        ),
    )(
        query_latent[0], query_rotary[0], key_latent[0], jnp.swapaxes(key_rotary[0], 0, 1), value_up,
        jnp.swapaxes(out_proj, 1, 2), residual[0], gain, out_grad[0], meta, gate_proj[0], up_proj[0], down_proj[0],
    )
    layer_out, resid_grad, score_grad = pl.pallas_call(
        functools.partial(final_kernel, K),
        name="finish",
        out_shape=(shape((tok, D), bf16), shape((tok, D), bf16), shape((tok, K), f32)),
        in_specs=[VM] * 7,
        out_specs=(VM,) * 3,
    )(hs, so, dn, wg, out_grad[0], meta, gain)
    return (layer_out[None], resid_grad[None], score_grad[None])


def solution(mesh):
    return jax.shard_map(
        functools.partial(per_device, mesh.shape["ctx"], mesh.shape["tp"]),
        mesh=mesh,
        in_specs=(
            P("dp", "ctx", "tp"),
            P("dp", "ctx", "tp"),
            P("dp", "ctx", None),
            P("dp", "ctx", None),
            P("tp", "ctx", None),
            P("tp", None, "ctx"),
            P("dp", ("ctx", "tp"), None),
            P(),
            P(("ctx", "tp"), "dp", None),
            P(("ctx", "tp"), "dp", None),
            P(("ctx", "tp"), "dp", None),
            P("dp", ("ctx", "tp"), None),
            P("dp", ("ctx", "tp"), None),
            P("dp", ("ctx", "tp"), None),
        ),
        out_specs=(
            P("dp", ("ctx", "tp"), None),
            P("dp", ("ctx", "tp"), None),
            P("dp", ("ctx", "tp"), None),
        ),
        check_vma=False,
    )
```

time: 530 us -> 237 us (0.45); the launches traced: 522 us -> 235 us
  waiting for transfers between devices: 325 us -> 0 us
  Pallas kernels: 0 us -> 231 us
  matrix products: 67.2 us -> 0 us
  local copies, waits for them, and re-layouts: 41.3 us -> 2.26 us
  starting transfers between devices: 31.9 us -> 0 us
  blocking collectives: 24.5 us -> 0 us
  between operations: 16.1 us -> 0.65 us
  other arithmetic: 15.6 us -> 1.36 us
    pallas_call x0 -> x2, Pallas kernels: none -> 231 us  [the longest x1 229 us: per_device(): pl.pallas_call(functools.partial(main_kernel, C, T, K, ND, NR), name='lay...]
    all_to_all x2 -> x0, waiting for transfers between devices: 163 us -> none  [the longest x1 82.3 us: per_device(): lax.all_to_all(outgoing, ('ctx', 'tp'), split_axis=0, concat_axis=0, tile...]
    all_gather x6 -> x0, waiting for transfers between devices: 135 us -> none  [the longest x1 73.1 us: per_device(): lax.all_gather(out_proj, 'ctx', axis=2, tiled=True)]
    dot_general x15 -> x0, matrix products: 67.2 us -> none  [the longest x1 7.28 us: expert_pass(): act_b = jnp.dot(rows_u, up_w, preferred_element_type=jnp.float32)]
    all_gather x1 -> x0, blocking collectives: 24.5 us -> none  [per_device(): lax.all_gather(key_rotary, 'ctx', axis=1, tiled=True)]
    reduce_scatter x1 -> x0, waiting for transfers between devices: 24.1 us -> none  [per_device(): lax.psum_scatter(jnp.dot(heads_out, flat_out, preferred_element_type=jnp....]
    all_to_all x2 -> x0, starting transfers between devices: 20 us -> none  [the longest x1 12.2 us: per_device(): lax.all_to_all(outgoing, ('ctx', 'tp'), split_axis=0, concat_axis=0, tile...]
    all_gather x6 -> x0, starting transfers between devices: 11.8 us -> none  [the longest x1 11.6 us: per_device(): lax.all_gather(up_proj, 'dp', axis=1, tiled=True)]
  transfers between devices with their start and end apart: 9 -> 0, of which waited for: 6 -> 0; matrix products, arithmetic and copies ran while one was open for 11% -> 0% of each run, Pallas kernels for 0% -> 0%
where the time goes in v2:
time: 237 us; the launch traced here: 235 us
  Pallas kernels  231 us (97%)
    pallas_call x1, Pallas kernels, per_device(): pl.pallas_call(functools.partial(main_kernel, C, T, K, ND, NR), name='lay...  229 us

profile of v2, /device:TPU:32, one launch (start us, length us, event | category | flops | bytes accessed | tf_op | source)
XLA Modules:
  0.0 235.1 jit_solution(13112916989915743988)
XLA Ops:
  0.6 0.1 pad.2.clone
  0.7 0.7 convert_bitcast_fusion
  1.4 0.1 copy.17
  1.5 0.8 copy.18
  2.2 0.7 maximum_maximum_fusion.meta
  2.9 228.7 %layer.1 = (f32[16,3584]{1,0:T(8,128)}, f32[16,3584]{1,0:T(8,128)}, f32[16,3584]{1,0:T(8,128)}, f32[16,128]{1,0:T(8,128)}) custom-call(bf16[128,4096]{1,0:T(8,128)(2,1)} %bitcast.22, bf16[128,512]{1,0:T(8,128)(2,1)} %bitcast.26, bf16[128,512]{1,0:T(8,128)(2,1)} %bitcast.27, bf16[64,128]{1,0:T(8,128)(2,1)} %bitcast.31, bf16[8,32,128]{2,1,0:T(8,128)(2,1)} %vs.1, ...), custom_call_target="tpu_custom_call" | custom-call | tf_op jit(solution)/shard_map/layer/pallas_call | solution.py:543
  231.7 2.1 finish.1
  233.8 1.4 copy.19
  (1 shorter events, 0.0 us)

commit v3 on v2

--- a/solution.py
+++ b/solution.py
@@ -51,6 +51,27 @@
     return jnp.concatenate([ref[i : i + 1, :] for i in range(ref.shape[0])], axis=1)
 
 
+def exact_tn(x, y):
+    return lax.dot_general(
+        x, y, (((0,), (0,)), ((), ())), preferred_element_type=f32, precision=lax.Precision.HIGHEST
+    )
+
+
+def exact_nt(x, y):
+    return lax.dot_general(
+        x, y, (((1,), (1,)), ((), ())), preferred_element_type=f32, precision=lax.Precision.HIGHEST
+    )
+
+
+def unit_rows(n, first):
+    at_row = lax.broadcasted_iota(jnp.int32, (n, LANES), 0) + first
+    return (lax.broadcasted_iota(jnp.int32, (n, LANES), 1) == at_row).astype(f32)
+
+
+def lanes_of(x, first):
+    return exact_tn(x, unit_rows(x.shape[0], first))
+
+
 def tour(n):
     if n == 4:
         return [(1, 0), (0, 1), (3, 0), (0, 3), (1, 1), (3, 3), (1, 3), (3, 1), (2, 0), (0, 2), (2, 1), (1, 2),
@@ -60,11 +81,11 @@
 
 def main_kernel(
     C, T, K, ND, NR,
-    ql, qr, kl, krt, vs, ost, res, gain, g, meta, gw, uw, dw,
+    ql, qr, kl, krt, vs, ost, res, gain, g, idt, sct, gw, uw, dw,
     hs_o, so_o, dn_o, wg_o,
     qbuf, kbuf, vbuf, obuf, us, ds_, heads, part, rsb, zm, zg, zu, sx, ag, au, act, ab, place, wts,
     ro, rd, rw, bo, bd, bw, pd, pw, fo, fd, fw,
-    wl, w_ss, w_rs, k_ss, k_rs, v_ss, v_rs, o_ss, o_rs, sv_ss, sv_rs, so_ss, so_rs, r_ss, r_rs,
+    wl, w_ss, w_rs, k_ss, k_rs, kz_ss, kz_rs, v_ss, v_rs, o_ss, o_rs, sv_ss, sv_rs, so_ss, so_rs, r_ss, r_rs,
     zm_ss, zm_rs, zg_ss, zg_rs, zu_ss, zu_rs, xg_ss, xg_rs, xu_ss, xu_rs, b_ss, b_rs, bw_ss, bw_rs,
     y_ss, y_rs, yw_ss, yw_rs, ready,
 ):
@@ -129,31 +150,30 @@
     swap_u = remote(uw, half_rows(us, d, DH), w_ss.at[1], w_rs.at[1], sib)
     swap_g = remote(gw, half_rows(gs, d, DH), w_ss.at[2], w_rs.at[2], sib)
 
-    def key_rows(i):
-        return kbuf.at[pl.ds(pl.multiple_of(i * rows, rows), rows)]
+    HR = rows // 2
+    side = lax.rem(t, 2)
+    mate = {"tp": t + 1 - 2 * side}
+
+    def key_half(i, h):
+        return kbuf.at[pl.ds(pl.multiple_of(i * rows + h * HR, HR), HR)]
+
+    def key_copy(owner, p):
+        return remote(key_half(owner, side), key_half(owner, side), k_ss.at[p], k_rs.at[owner], {"ctx": p})
+
+    def key_pass(owner, h):
+        return remote(key_half(owner, h), key_half(owner, h), kz_ss.at[owner], kz_rs.at[owner], mate)
 
     my_keys = pl.ds(pl.multiple_of(c * rows, rows), rows)
     kbuf[my_keys, 0:LAT] = kl[...]
     kr = tn(krt[...], identity(ROPE)).astype(bf16)
     kbuf[my_keys, LAT:KW] = jnp.concatenate([kr, jnp.zeros((rows, KW - LAT - ROPE), bf16)], axis=1)
-    zm[t] = meta[...]
+    zm[t] = lanes_of(idt[...].astype(f32), 0) + lanes_of(sct[...], K)
     zg[t] = g[...]
-    pl.semaphore_wait(bar, C + T - 1)
-
-    def send_keys(p):
-        @pl.when(p > c)
-        def _():
-            remote(key_rows(c), key_rows(c), k_ss.at[p], k_rs.at[c], {"ctx": p}).start()
-
-    to_xy(send_keys)
-    to_z(lambda p: remote(zm.at[t], zm.at[t], zm_ss.at[p], zm_rs.at[t], {"tp": p}).start())
-    to_z(lambda p: remote(zg.at[t], zg.at[t], zg_ss.at[p], zg_rs.at[t], {"tp": p}).start())
-    swap_d.start()
-    swap_u.start()
-
     for h in range(H):
         obuf[pl.ds(pl.multiple_of(c * OC, OC), OC), h * VD : (h + 1) * VD] = ost[h]
     vbuf[:, pl.ds(pl.multiple_of(c * LR, LR), LR), :] = vs[...]
+    pl.semaphore_wait(bar, C + T - 1)
+
 
     def v_part(owner, half):
         return vbuf.at[pl.ds(half * Hh, Hh), pl.ds(pl.multiple_of(owner * LR, LR), LR), :]
@@ -184,6 +204,21 @@
     def wait_send(copies):
         for x in copies:
             x.wait_send()
+
+    for o in range(1, NX):
+        start(vo(c, o, at(o, 0)))
+
+    def send_keys(p):
+        @pl.when(p > c)
+        def _():
+            key_copy(c, p).start()
+
+    to_xy(send_keys)
+    for o in range(1, NX):
+        start(vo(c, NX + o, at(0, o)))
+    to_z(lambda p: remote(zm.at[t], zm.at[t], zm_ss.at[p], zm_rs.at[t], {"tp": p}).start())
+    swap_d.start()
+    swap_u.start()
 
     def blank(j):
         kbuf[pl.ds(pl.multiple_of(j * rows, rows), rows), :] = jnp.zeros((rows, KW), bf16)
@@ -195,13 +230,6 @@
             [qr[:, h * ROPE : (h + 1) * ROPE], jnp.zeros((rows, KW - LAT - ROPE), bf16)], axis=1
         )
 
-    each(0, c, lambda j: remote(key_rows(j), key_rows(j), k_ss.at[j], k_rs.at[j], {"ctx": j}).wait_recv())
-
-    for o in range(1, NX):
-        start(vo(c, o, at(o, 0)))
-    for o in range(1, NX):
-        start(vo(c, NX + o, at(0, o)))
-
     def pass_on(i):
         owner = lax.rem(a + NX - i, NX) * sa + b * sb
         wait_recv(vo(owner, 0, owner))
@@ -209,6 +237,17 @@
             start(vo(owner, NX * (i + 1) + o, at(0, o)))
         start(vo_relay(owner, d))
 
+    for i in (1, 3, 2) if NX == 4 else range(1, NX):
+        pass_on(i)
+
+    def key_relay(j):
+        key_copy(j, j).wait_recv()
+        key_pass(j, side).start()
+
+    each(0, c, key_relay)
+    to_z(lambda p: remote(zg.at[t], zg.at[t], zg_ss.at[p], zg_rs.at[t], {"tp": p}).start())
+    each(0, c, lambda j: key_pass(j, 1 - side).wait_recv())
+
     S = C * rows
     NB = 4
     SN = S // NB
@@ -218,10 +257,6 @@
         return act.at[n // 2, 0:MB, (n % 2) * SN : (n % 2 + 1) * SN]
 
     def attend(i):
-        @pl.when(jnp.logical_and(i > 0, i < NX))
-        def _():
-            pass_on(i)
-
         r = pl.ds(pl.multiple_of(i * MB, MB), MB)
         q = qbuf[r, :]
         qpos = c * rows + lax.rem(lax.broadcasted_iota(jnp.int32, (MB, SN), 0), rows)
@@ -304,15 +339,20 @@
     for h in range(H):
         heads[:, h * VD : (h + 1) * VD] = nn(qbuf[h * rows : (h + 1) * rows, 0:LAT], vbuf[h]).astype(bf16)
 
-    PN = 512 if D % 512 == 0 else D
+    def u_cols(n):
+        return pl.ds(pl.multiple_of(n * CD, CD), CD)
+
+    def partial(n, p, q):
+        cols = u_cols(n)
+        return remote(part.at[p, :, cols], rsb.at[q, :, cols], r_ss.at[n, p], r_rs.at[n, q], {"tp": p})
 
     def project(n):
-        cols = pl.ds(pl.multiple_of(n * PN, PN), PN)
-        part[:, :, cols] = nt(heads[...], obuf[cols, :]).astype(bf16).reshape(T, tok, PN)
-
-    each(0, D // PN, project)
-    to_z(lambda p: remote(part.at[p], rsb.at[t], r_ss.at[p], r_rs.at[t], {"tp": p}).start())
-    rsb[t] = part[t]
+        cols = u_cols(n)
+        part[:, :, cols] = nt(heads[...], obuf[cols, :]).astype(bf16).reshape(T, tok, CD)
+        to_z(lambda p: partial(n, p, t).start())
+        rsb[t, :, cols] = part[t, :, cols]
+
+    each(0, ND, project)
 
     def sent_vo(off):
         for o in range(1, NX):
@@ -323,7 +363,7 @@
     pl.semaphore_signal(ready, inc=1, device_id=sib, device_id_type=MESH)
     own_g.start()
 
-    from_z(lambda p: remote(part.at[p], rsb.at[p], r_ss.at[p], r_rs.at[p], {"tp": p}).wait_recv())
+    each(0, ND, lambda n: from_z(lambda p: partial(n, p, p).wait_recv()))
     hs = rsb[0].astype(f32)
     for i in range(1, T):
         hs = hs + rsb[i].astype(f32)
@@ -331,9 +371,6 @@
     hs_o[...] = hs
     inv = lax.rsqrt(jnp.mean(hs * hs, axis=1, keepdims=True) + norm_eps)
     zu[t] = (hs * inv * row_of(gain)).astype(bf16)
-
-    def u_cols(n):
-        return pl.ds(pl.multiple_of(n * CD, CD), CD)
 
     def z_u(n, p, q):
         cols = u_cols(n)
@@ -431,7 +468,7 @@
 
     each(0, NR, grads)
 
-    to_z(lambda p: remote(part.at[p], rsb.at[t], r_ss.at[p], r_rs.at[t], {"tp": p}).wait_send())
+    each(0, ND, lambda n: to_z(lambda p: partial(n, p, t).wait_send()))
     sums = ((part, fo), (pd, fd))
 
     def z_back(i, n, p, q):
@@ -487,7 +524,8 @@
     for i in range(2):
         each(0, NR, lambda n: from_xy(lambda p: back(i, n, p, c).wait_send()))
     from_xy(lambda p: w_back(p, c).wait_send())
-    each(c + 1, C, lambda j: remote(key_rows(c), key_rows(c), k_ss.at[j], k_rs.at[c], {"ctx": j}).wait_send())
+    each(c + 1, C, lambda j: key_copy(c, j).wait_send())
+    each(0, c, lambda j: key_pass(j, side).wait_send())
 
     each(0, NR, lambda n: from_z(lambda p: z_back(1, n, p, p).wait_recv()))
     dn_o[...] = total_of(fd)
@@ -496,13 +534,13 @@
         each(0, NR, lambda n: to_z(lambda p: z_back(i, n, p, t).wait_send()))
 
 
-def final_kernel(K, hs, so, dn, wg, g, meta, gain, lo_o, rg_o, sg_o):
+def final_kernel(K, hs, so, dn, wg, g, sct, gain, lo_o, rg_o, sg_o):
     h = hs[...]
     lo_o[...] = (h + so[...]).astype(bf16)
-    wgt = wg[:, 0:K]
-    sc = meta[:, K : 2 * K]
-    st = jnp.sum(sc, axis=1, keepdims=True)
-    sg_o[...] = route_scale / st * (wgt - jnp.sum(wgt * sc, axis=1, keepdims=True) / st)
+    wgt = exact_nt(unit_rows(K, 0), wg[...])
+    sc = sct[...]
+    st = jnp.sum(sc, axis=0, keepdims=True)
+    sg_o[...] = route_scale / st * (wgt - jnp.sum(wgt * sc, axis=0, keepdims=True) / st)
     dng = dn[...] * row_of(gain)
     inv = lax.rsqrt(jnp.mean(h * h, axis=1, keepdims=True) + norm_eps)
     proj = jnp.mean(dng * h, axis=1, keepdims=True)
@@ -531,9 +569,8 @@
     NX = math.isqrt(C)
     ND, NR = 4, 4
     gain = norm_gain.reshape(D // LANES, LANES)
-    meta = jnp.concatenate(
-        [expert_ids[0].astype(f32), route_score[0], jnp.zeros((tok, LANES - 2 * K), f32)], axis=1
-    )
+    id_t = jnp.swapaxes(expert_ids[0], 0, 1)
+    score_t = jnp.swapaxes(route_score[0], 0, 1)
     dma = pltpu.SemaphoreType.DMA
     shape = jax.ShapeDtypeStruct
     vmem = pltpu.VMEM
@@ -544,7 +581,7 @@
         functools.partial(main_kernel, C, T, K, ND, NR),
         name="layer",
         out_shape=(shape((tok, D), f32), shape((tok, D), f32), shape((tok, D), f32), shape((tok, LANES), f32)),
-        in_specs=[VM] * 10 + [ANY] * 3,
+        in_specs=[VM] * 11 + [ANY] * 3,
         out_specs=(VM,) * 4,
         scratch_shapes=[
             vmem((H * rows, KW), bf16),
@@ -565,10 +602,10 @@
             vmem(zz, bf16), vmem((T, tok, LANES), f32),
             vmem(zz, bf16), vmem(zz, bf16), vmem((T, tok, LANES), f32),
             dma((3,)), dma((3,)), dma((3,)),
-            dma((C,)), dma((C,)),
+            dma((C,)), dma((C,)), dma((C,)), dma((C,)),
             dma((NX * (NX + 1),)), dma((C,)), dma((NX * (NX + 1),)), dma((C,)),
             dma((C,)), dma((C,)), dma((C,)), dma((C,)),
-            dma((T,)), dma((T,)),
+            dma((ND, T)), dma((ND, T)),
             dma((T,)), dma((T,)), dma((T,)), dma((T,)), dma((ND, T)), dma((ND, T)),
             dma((2, C)), dma((2, C)), dma((ND, C)), dma((ND, C)),
             dma((2 * NR, C)), dma((2 * NR, C)), dma((C,)), dma((C,)),
@@ -580,16 +617,17 @@
         ),
     )(
         query_latent[0], query_rotary[0], key_latent[0], jnp.swapaxes(key_rotary[0], 0, 1), value_up,
-        jnp.swapaxes(out_proj, 1, 2), residual[0], gain, out_grad[0], meta, gate_proj[0], up_proj[0], down_proj[0],
+        jnp.swapaxes(out_proj, 1, 2), residual[0], gain, out_grad[0], id_t, score_t, gate_proj[0], up_proj[0],
+        down_proj[0],
     )
     layer_out, resid_grad, score_grad = pl.pallas_call(
         functools.partial(final_kernel, K),
         name="finish",
-        out_shape=(shape((tok, D), bf16), shape((tok, D), bf16), shape((tok, K), f32)),
+        out_shape=(shape((tok, D), bf16), shape((tok, D), bf16), shape((K, tok), f32)),
         in_specs=[VM] * 7,
         out_specs=(VM,) * 3,
-    )(hs, so, dn, wg, out_grad[0], meta, gain)
-    return (layer_out[None], resid_grad[None], score_grad[None])
+    )(hs, so, dn, wg, out_grad[0], score_t, gain)
+    return (layer_out[None], resid_grad[None], jnp.swapaxes(score_grad, 0, 1)[None])
 
 
 def solution(mesh):

time: 237 us -> 215 us (0.907)
  Pallas kernels: 231 us -> 214 us
    pallas_call x1, Pallas kernels: 229 us -> 211 us  [per_device(): pl.pallas_call(functools.partial(main_kernel, C, T, K, ND, NR), name='lay...]
where the time goes in v3:
time: 215 us; the launch traced here: 214 us
  Pallas kernels  214 us (100%)
    pallas_call x1, Pallas kernels, per_device(): pl.pallas_call(functools.partial(main_kernel, C, T, K, ND, NR), name='lay...  211 us

profile of v3, /device:TPU:32, one launch (start us, length us, event | category | flops | bytes accessed | tf_op | source)
XLA Modules:
  0.0 214.2 jit_solution(17346444786570182668)
XLA Ops:
  0.6 211.5 %layer.1 = (f32[16,3584]{1,0:T(8,128)}, f32[16,3584]{1,0:T(8,128)}, f32[16,3584]{1,0:T(8,128)}, f32[16,128]{1,0:T(8,128)}) custom-call(bf16[128,4096]{1,0:T(8,128)(2,1)} %bitcast.27, bf16[128,512]{1,0:T(8,128)(2,1)} %bitcast.31, bf16[128,512]{1,0:T(8,128)(2,1)} %bitcast.32, bf16[64,128]{1,0:T(8,128)(2,1)} %bitcast.36, bf16[8,32,128]{2,1,0:T(8,128)(2,1)} %vs.1, ...), custom_call_target="tpu_custom_call" | custom-call | tf_op jit(solution)/shard_map/layer/pallas_call | solution.py:580
  212.1 2.1 finish.1

commit v4 on v3

--- a/solution.py
+++ b/solution.py
@@ -150,18 +150,18 @@
     swap_u = remote(uw, half_rows(us, d, DH), w_ss.at[1], w_rs.at[1], sib)
     swap_g = remote(gw, half_rows(gs, d, DH), w_ss.at[2], w_rs.at[2], sib)
 
-    HR = rows // 2
+    ZR = rows * 3 // 8
+    XR = rows - ZR
     side = lax.rem(t, 2)
     mate = {"tp": t + 1 - 2 * side}
 
-    def key_half(i, h):
-        return kbuf.at[pl.ds(pl.multiple_of(i * rows + h * HR, HR), HR)]
-
     def key_copy(owner, p):
-        return remote(key_half(owner, side), key_half(owner, side), k_ss.at[p], k_rs.at[owner], {"ctx": p})
+        ref = kbuf.at[pl.ds(pl.multiple_of(owner * rows + side * ZR, math.gcd(rows, ZR)), XR)]
+        return remote(ref, ref, k_ss.at[p], k_rs.at[owner], {"ctx": p})
 
     def key_pass(owner, h):
-        return remote(key_half(owner, h), key_half(owner, h), kz_ss.at[owner], kz_rs.at[owner], mate)
+        ref = kbuf.at[pl.ds(pl.multiple_of(owner * rows + h * XR, math.gcd(rows, XR)), ZR)]
+        return remote(ref, ref, kz_ss.at[owner], kz_rs.at[owner], mate)
 
     my_keys = pl.ds(pl.multiple_of(c * rows, rows), rows)
     kbuf[my_keys, 0:LAT] = kl[...]
@@ -214,11 +214,7 @@
             key_copy(c, p).start()
 
     to_xy(send_keys)
-    for o in range(1, NX):
-        start(vo(c, NX + o, at(0, o)))
     to_z(lambda p: remote(zm.at[t], zm.at[t], zm_ss.at[p], zm_rs.at[t], {"tp": p}).start())
-    swap_d.start()
-    swap_u.start()
 
     def blank(j):
         kbuf[pl.ds(pl.multiple_of(j * rows, rows), rows), :] = jnp.zeros((rows, KW), bf16)
@@ -237,16 +233,17 @@
             start(vo(owner, NX * (i + 1) + o, at(0, o)))
         start(vo_relay(owner, d))
 
-    for i in (1, 3, 2) if NX == 4 else range(1, NX):
-        pass_on(i)
-
     def key_relay(j):
         key_copy(j, j).wait_recv()
         key_pass(j, side).start()
 
     each(0, c, key_relay)
+    for o in range(1, NX):
+        start(vo(c, NX + o, at(0, o)))
+    for i in (1, 3, 2) if NX == 4 else range(1, NX):
+        pass_on(i)
+    each(0, c, lambda j: key_pass(j, 1 - side).wait_recv())
     to_z(lambda p: remote(zg.at[t], zg.at[t], zg_ss.at[p], zg_rs.at[t], {"tp": p}).start())
-    each(0, c, lambda j: key_pass(j, 1 - side).wait_recv())
 
     S = C * rows
     NB = 4
@@ -335,6 +332,8 @@
     each(0, 2, lambda n: to_xy(lambda p: xg(n, p, c).start()))
 
     from_xy(lambda p: wait_recv(vo_relay(p, 1 - d)))
+    swap_d.start()
+    swap_u.start()
 
     for h in range(H):
         heads[:, h * VD : (h + 1) * VD] = nn(qbuf[h * rows : (h + 1) * rows, 0:LAT], vbuf[h]).astype(bf16)

time: 215 us -> 219 us (1.019)
  Pallas kernels: 214 us -> 217 us
    pallas_call x1, Pallas kernels: 211 us -> 215 us  [per_device(): pl.pallas_call(functools.partial(main_kernel, C, T, K, ND, NR), name='lay...]
where the time goes in v4:
time: 219 us; the launch traced here: 218 us
  Pallas kernels  217 us (99%)
    pallas_call x1, Pallas kernels, per_device(): pl.pallas_call(functools.partial(main_kernel, C, T, K, ND, NR), name='lay...  215 us

profile of v4, /device:TPU:32, one launch (start us, length us, event | category | flops | bytes accessed | tf_op | source)
XLA Modules:
  0.0 217.7 jit_solution(5747447316620550844)
XLA Ops:
  0.6 215.0 %layer.1 = (f32[16,3584]{1,0:T(8,128)}, f32[16,3584]{1,0:T(8,128)}, f32[16,3584]{1,0:T(8,128)}, f32[16,128]{1,0:T(8,128)}) custom-call(bf16[128,4096]{1,0:T(8,128)(2,1)} %bitcast.27, bf16[128,512]{1,0:T(8,128)(2,1)} %bitcast.31, bf16[128,512]{1,0:T(8,128)(2,1)} %bitcast.32, bf16[64,128]{1,0:T(8,128)(2,1)} %bitcast.36, bf16[8,32,128]{2,1,0:T(8,128)(2,1)} %vs.1, ...), custom_call_target="tpu_custom_call" | custom-call | tf_op jit(solution)/shard_map/layer/pallas_call | solution.py:579
  215.6 2.1 finish.1

commit v5 on v4

--- a/solution.py
+++ b/solution.py
@@ -85,7 +85,7 @@
     hs_o, so_o, dn_o, wg_o,
     qbuf, kbuf, vbuf, obuf, us, ds_, heads, part, rsb, zm, zg, zu, sx, ag, au, act, ab, place, wts,
     ro, rd, rw, bo, bd, bw, pd, pw, fo, fd, fw,
-    wl, w_ss, w_rs, k_ss, k_rs, kz_ss, kz_rs, v_ss, v_rs, o_ss, o_rs, sv_ss, sv_rs, so_ss, so_rs, r_ss, r_rs,
+    wl, w_ss, w_rs, k_ss, k_rs, v_ss, v_rs, o_ss, o_rs, sv_ss, sv_rs, so_ss, so_rs, r_ss, r_rs,
     zm_ss, zm_rs, zg_ss, zg_rs, zu_ss, zu_rs, xg_ss, xg_rs, xu_ss, xu_rs, b_ss, b_rs, bw_ss, bw_rs,
     y_ss, y_rs, yw_ss, yw_rs, ready,
 ):
@@ -150,18 +150,32 @@
     swap_u = remote(uw, half_rows(us, d, DH), w_ss.at[1], w_rs.at[1], sib)
     swap_g = remote(gw, half_rows(gs, d, DH), w_ss.at[2], w_rs.at[2], sib)
 
-    ZR = rows * 3 // 8
-    XR = rows - ZR
-    side = lax.rem(t, 2)
-    mate = {"tp": t + 1 - 2 * side}
-
-    def key_copy(owner, p):
-        ref = kbuf.at[pl.ds(pl.multiple_of(owner * rows + side * ZR, math.gcd(rows, ZR)), XR)]
-        return remote(ref, ref, k_ss.at[p], k_rs.at[owner], {"ctx": p})
-
-    def key_pass(owner, h):
-        ref = kbuf.at[pl.ds(pl.multiple_of(owner * rows + h * XR, math.gcd(rows, XR)), ZR)]
-        return remote(ref, ref, kz_ss.at[owner], kz_rs.at[owner], mate)
+    def key_copy(owner, i, p):
+        ref = kbuf.at[pl.ds(pl.multiple_of(owner * rows, rows), rows)]
+        return remote(ref, ref, k_ss.at[i], k_rs.at[owner], {"ctx": p})
+
+    def y_of(pa, pb):
+        return pb * (1 - d) + pa * d
+
+    def first_hops(fn):
+        for o in range(1, NX):
+            @pl.when(row <= y_of(lax.rem(a + o, NX), b))
+            def _():
+                fn(key_copy(c, o, at(o, 0)))
+
+    def second_hops(i, fn):
+        oa = lax.rem(a + NX - i, NX)
+        for o in range(1, NX):
+            @pl.when(y_of(oa, b) <= y_of(a, lax.rem(b + o, NX)))
+            def _():
+                fn(key_copy(oa * sa + b * sb, NX * (i + 1) + o, at(0, o)))
+
+    def key_in(oa, ob):
+        owner = oa * sa + ob * sb
+
+        @pl.when(y_of(oa, ob) <= row)
+        def _():
+            key_copy(owner, 0, owner).wait_recv()
 
     my_keys = pl.ds(pl.multiple_of(c * rows, rows), rows)
     kbuf[my_keys, 0:LAT] = kl[...]
@@ -208,18 +222,15 @@
     for o in range(1, NX):
         start(vo(c, o, at(o, 0)))
 
-    def send_keys(p):
-        @pl.when(p > c)
-        def _():
-            key_copy(c, p).start()
-
-    to_xy(send_keys)
+    first_hops(lambda x: x.start())
+    second_hops(0, lambda x: x.start())
     to_z(lambda p: remote(zm.at[t], zm.at[t], zm_ss.at[p], zm_rs.at[t], {"tp": p}).start())
+    to_z(lambda p: remote(zg.at[t], zg.at[t], zg_ss.at[p], zg_rs.at[t], {"tp": p}).start())
 
     def blank(j):
         kbuf[pl.ds(pl.multiple_of(j * rows, rows), rows), :] = jnp.zeros((rows, KW), bf16)
 
-    each(c + 1, C, blank)
+    each((row + 1) * NX, C, blank)
     for h in range(H):
         qbuf[h * rows : (h + 1) * rows, 0:LAT] = ql[:, h * LAT : (h + 1) * LAT]
         qbuf[h * rows : (h + 1) * rows, LAT:KW] = jnp.concatenate(
@@ -233,17 +244,15 @@
             start(vo(owner, NX * (i + 1) + o, at(0, o)))
         start(vo_relay(owner, d))
 
-    def key_relay(j):
-        key_copy(j, j).wait_recv()
-        key_pass(j, side).start()
-
-    each(0, c, key_relay)
+    for i in (1, 3, 2) if NX == 4 else range(1, NX):
+        key_in(lax.rem(a + NX - i, NX), b)
+        second_hops(i, lambda x: x.start())
     for o in range(1, NX):
         start(vo(c, NX + o, at(0, o)))
     for i in (1, 3, 2) if NX == 4 else range(1, NX):
         pass_on(i)
-    each(0, c, lambda j: key_pass(j, 1 - side).wait_recv())
-    to_z(lambda p: remote(zg.at[t], zg.at[t], zg_ss.at[p], zg_rs.at[t], {"tp": p}).start())
+    for o in range(1, NX):
+        each(0, NX, lambda oa: key_in(oa, lax.rem(b + o, NX)))
 
     S = C * rows
     NB = 4
@@ -523,8 +532,9 @@
     for i in range(2):
         each(0, NR, lambda n: from_xy(lambda p: back(i, n, p, c).wait_send()))
     from_xy(lambda p: w_back(p, c).wait_send())
-    each(c + 1, C, lambda j: key_copy(c, j).wait_send())
-    each(0, c, lambda j: key_pass(j, side).wait_send())
+    first_hops(lambda x: x.wait_send())
+    for i in range(NX):
+        second_hops(i, lambda x: x.wait_send())
 
     each(0, NR, lambda n: from_z(lambda p: z_back(1, n, p, p).wait_recv()))
     dn_o[...] = total_of(fd)
@@ -601,7 +611,7 @@
             vmem(zz, bf16), vmem((T, tok, LANES), f32),
             vmem(zz, bf16), vmem(zz, bf16), vmem((T, tok, LANES), f32),
             dma((3,)), dma((3,)), dma((3,)),
-            dma((C,)), dma((C,)), dma((C,)), dma((C,)),
+            dma((NX * (NX + 1),)), dma((C,)),
             dma((NX * (NX + 1),)), dma((C,)), dma((NX * (NX + 1),)), dma((C,)),
             dma((C,)), dma((C,)), dma((C,)), dma((C,)),
             dma((ND, T)), dma((ND, T)),

time: 219 us -> 212 us (0.968)
  Pallas kernels: 217 us -> 211 us
    pallas_call x1, Pallas kernels: 215 us -> 209 us  [per_device(): pl.pallas_call(functools.partial(main_kernel, C, T, K, ND, NR), name='lay...]
where the time goes in v5:
time: 212 us
  Pallas kernels  211 us (100%)
    pallas_call x1, Pallas kernels, per_device(): pl.pallas_call(functools.partial(main_kernel, C, T, K, ND, NR), name='lay...  209 us

profile of v5, /device:TPU:32, one launch (start us, length us, event | category | flops | bytes accessed | tf_op | source)
XLA Modules:
  0.0 211.6 jit_solution(1965172913898572925)
XLA Ops:
  0.6 208.8 %layer.1 = (f32[16,3584]{1,0:T(8,128)}, f32[16,3584]{1,0:T(8,128)}, f32[16,3584]{1,0:T(8,128)}, f32[16,128]{1,0:T(8,128)}) custom-call(bf16[128,4096]{1,0:T(8,128)(2,1)} %bitcast.27, bf16[128,512]{1,0:T(8,128)(2,1)} %bitcast.31, bf16[128,512]{1,0:T(8,128)(2,1)} %bitcast.32, bf16[64,128]{1,0:T(8,128)(2,1)} %bitcast.36, bf16[8,32,128]{2,1,0:T(8,128)(2,1)} %vs.1, ...), custom_call_target="tpu_custom_call" | custom-call | tf_op jit(solution)/shard_map/layer/pallas_call | solution.py:589
  209.5 2.1 finish.1

commit v6 on v5

--- a/solution.py
+++ b/solution.py
@@ -576,7 +576,7 @@
     NS = C * SL
     NT = T * tok
     NX = math.isqrt(C)
-    ND, NR = 4, 4
+    ND, NR = (7, 7) if D % (7 * LANES) == 0 else (4, 4)
     gain = norm_gain.reshape(D // LANES, LANES)
     id_t = jnp.swapaxes(expert_ids[0], 0, 1)
     score_t = jnp.swapaxes(route_score[0], 0, 1)

time: 212 us -> 217 us (1.024)
  Pallas kernels: 211 us -> 214 us
    pallas_call x1, Pallas kernels: 209 us -> 212 us  [per_device(): pl.pallas_call(functools.partial(main_kernel, C, T, K, ND, NR), name='lay...]
where the time goes in v6:
time: 217 us; the launch traced here: 214 us
  Pallas kernels  214 us (99%)
    pallas_call x1, Pallas kernels, per_device(): pl.pallas_call(functools.partial(main_kernel, C, T, K, ND, NR), name='lay...  212 us

profile of v6, /device:TPU:32, one launch (start us, length us, event | category | flops | bytes accessed | tf_op | source)
XLA Modules:
  0.0 214.4 jit_solution(5146601116415740076)
XLA Ops:
  0.6 211.7 %layer.1 = (f32[16,3584]{1,0:T(8,128)}, f32[16,3584]{1,0:T(8,128)}, f32[16,3584]{1,0:T(8,128)}, f32[16,128]{1,0:T(8,128)}) custom-call(bf16[128,4096]{1,0:T(8,128)(2,1)} %bitcast.27, bf16[128,512]{1,0:T(8,128)(2,1)} %bitcast.31, bf16[128,512]{1,0:T(8,128)(2,1)} %bitcast.32, bf16[64,128]{1,0:T(8,128)(2,1)} %bitcast.36, bf16[8,32,128]{2,1,0:T(8,128)(2,1)} %vs.1, ...), custom_call_target="tpu_custom_call" | custom-call | tf_op jit(solution)/shard_map/layer/pallas_call | solution.py:589
  212.3 2.1 finish.1
